TPU v7x, 32 devices: a whole 2x2x4 slice. The times are simulated.
32 devices in a mesh: groups: 2 (over x), ctx: 16 (over z, y, core).
Axes of the slice: x: 2, y: 2, z: 4, core: 2. Of those that a mesh axis runs over, the one named last changes fastest.
Arguments:
- query: bfloat16 [8192, 1024], P(('groups', 'ctx')), parts along dimension 0, may hold values from -130 to 130, as said below
- key: bfloat16 [8192, 1024], P(('groups', 'ctx')), parts along dimension 0, may hold values from -4.5 to 4.5
- value: bfloat16 [8192, 1024], P(('groups', 'ctx')), parts along dimension 0, may hold values from -6 to 6
- cotangent: bfloat16 [8192, 1024], P(('groups', 'ctx')), parts along dimension 0, may hold values from -6 to 6
- global_ids: int32 [4], P('groups'), parts along dimension 0, may hold values from 0 to 63
- rand_owner: int32 [128, 6], P('groups'), parts along dimension 0, may hold values from 0 to 15, all different within a row; in each aligned block of 4 rows (0 to 3, 4 to 7, ...) at most 2 rows name the same one
- rand_local: int32 [128, 6], P('groups'), parts along dimension 0, may hold values from 0 to 3
Outputs:
- attended: bfloat16 [8192, 1024], P(('groups', 'ctx')), parts along dimension 0
- grad_query: bfloat16 [8192, 1024], P(('groups', 'ctx')), parts along dimension 0
- grad_key: bfloat16 [8192, 1024], P(('groups', 'ctx')), parts along dimension 0
- grad_value: bfloat16 [8192, 1024], P(('groups', 'ctx')), parts along dimension 0
There are 2 independent parts, one for each index of `groups`. A program takes and returns all parts, laid end to end along the dimension named above; each array names one. Nothing has to cross between parts.
Inputs may be any that keep to these rules, and one draw needn't show every extreme that they name: query and key are drawn together. `rand_owner`: each row names 6 different devices. In the 4 rows of one device no device is named more than 2 times, and in some device's rows some device is named exactly 2 times.
All inputs are finite; a program needn't handle non-finite values.
Results may differ from a plain program's by a relative error of at most 0.017.
Values may be sent and summed in bfloat16 or wider, within the bound.
A program may use at most 192 MiB of HBM per device.

v0:
```python
import jax
import jax.numpy as jnp
from jax import lax
from jax.sharding import PartitionSpec as P

HEAD_DIM = 64
GROUP_HEADS = 8
BLOCK = 64
GLOBALS = 2
ROUNDS = 3


NEG_FILL = -1e30


def padded_2(block, sides, width):
    for axis, dim in sides:
        count = lax.axis_size(axis)
        forward = [(i, i + 1) for i in range(count - 1)]
        backward = [(target, source) for source, target in forward]
        low = lax.ppermute(
            lax.slice_in_dim(block, block.shape[dim] - width, None, axis=dim), axis, forward
        )
        high = lax.ppermute(lax.slice_in_dim(block, 0, width, axis=dim), axis, backward)
        block = jnp.concatenate([low, block, high], axis=dim)
    return block


def broadcast(array, axis, root):
    mine = lax.axis_index(axis) == root
    return lax.psum(jnp.where(mine, array, jnp.zeros_like(array)), axis)


def request_ranks(owners, device_count):
    onehot = (owners[:, :, None] == jnp.arange(device_count, dtype=jnp.int32)).astype(jnp.int32)
    before = jnp.cumsum(onehot, axis=1) - onehot
    return jnp.sum(before * onehot, axis=2)


def per_device(query, key, value, cotangent, global_ids, rand_owner, rand_local):
    tok_count, features = query.shape
    blocks = tok_count // BLOCK
    head_count = features // HEAD_DIM
    groups = head_count // GROUP_HEADS
    group_width = GROUP_HEADS * HEAD_DIM
    device_count = lax.axis_size("ctx")
    my_index = lax.axis_index("ctx")
    pick_count = groups * ROUNDS
    slot_count = max(2, (pick_count * blocks + device_count - 1) // device_count)
    score_scale = HEAD_DIM ** (-0.5)
    key_kinds = 3 + GLOBALS + ROUNDS
    key_span = key_kinds * BLOCK
    kv_local = jnp.stack(
        (key.reshape(blocks, BLOCK, features), value.reshape(blocks, BLOCK, features)), axis=2
    )
    padded = padded_2(kv_local, (("ctx", 0),), 1)
    glob_list = []
    for glob_index in range(GLOBALS):
        root_dev = global_ids[glob_index] // blocks
        local_block = global_ids[glob_index] % blocks
        block_kv = lax.dynamic_index_in_dim(kv_local, local_block, 0, keepdims=False)
        glob_list.append(broadcast(block_kv, "ctx", root_dev))
    glob_kv = jnp.stack(glob_list)
    owners_all = rand_owner.reshape(device_count, blocks * pick_count)
    locals_all = rand_local.reshape(device_count, blocks * pick_count)
    ranks_all = request_ranks(owners_all, device_count)
    my_owner = lax.dynamic_index_in_dim(owners_all, my_index, 0, keepdims=False)
    my_rank = lax.dynamic_index_in_dim(ranks_all, my_index, 0, keepdims=False)
    fetch_index = my_owner * slot_count + my_rank
    entry_group = jnp.arange(blocks * pick_count, dtype=jnp.int32) % pick_count // ROUNDS
    matched = (
        (owners_all[:, :, None] == my_index)
        & (ranks_all[:, :, None] == jnp.arange(slot_count, dtype=jnp.int32))
    ).astype(jnp.int32)
    send_block = jnp.sum(matched * locals_all[:, :, None], axis=1).reshape(-1)
    send_group = jnp.sum(matched * entry_group[None, :, None], axis=1).reshape(-1)
    send_live = jnp.sum(matched, axis=1).reshape(-1) > 0
    kv_grouped = kv_local.reshape(blocks, BLOCK, 2, groups, group_width)

    def pack_blocks():
        picked = kv_grouped[send_block, :, :, send_group, :]
        picked = jnp.where(send_live[:, None, None, None], picked, jnp.zeros((), picked.dtype))
        return picked.reshape(device_count, slot_count, BLOCK, 2, group_width)

    def unpack_blocks(arrived):
        arrived_flat = arrived.reshape(device_count * slot_count, BLOCK, 2, group_width)
        return arrived_flat[fetch_index].reshape(blocks, groups, ROUNDS, BLOCK, 2, group_width)

    random_kv = unpack_blocks(
        lax.all_to_all(pack_blocks(), "ctx", split_axis=0, concat_axis=0, tiled=True)
    )
    block_ids = jnp.arange(blocks)
    left_ok = jnp.logical_or(my_index > 0, block_ids > 0)
    right_ok = jnp.logical_or(my_index < device_count - 1, block_ids < blocks - 1)
    key_valid = jnp.concatenate(
        (
            jnp.repeat(left_ok[:, None], BLOCK, axis=1),
            jnp.ones((blocks, BLOCK), jnp.bool_),
            jnp.repeat(right_ok[:, None], BLOCK, axis=1),
            jnp.ones((blocks, (GLOBALS + ROUNDS) * BLOCK), jnp.bool_),
        ),
        axis=1,
    )
    valid_four = key_valid[:, None, None, :]

    def assemble(group_idx, source_kv):
        start_col = group_idx * group_width
        window = jnp.stack(
            [
                padded[offset : offset + blocks, :, :, start_col : start_col + group_width]
                for offset in range(3)
            ],
            axis=1,
        )
        global_part = jnp.broadcast_to(
            glob_kv[None, :, :, :, start_col : start_col + group_width],
            (blocks, GLOBALS, BLOCK, 2, group_width),
        )
        random_part = source_kv[:, group_idx]
        joined = jnp.concatenate((window, global_part, random_part), axis=1)
        joined = joined.reshape(blocks, key_span, 2, GROUP_HEADS, HEAD_DIM)
        return (joined[:, :, 0], joined[:, :, 1])

    def score_block(query_group, keys_group):
        scores = (
            jnp.einsum(
                "bqhd,bkhd->bhqk", query_group, keys_group, preferred_element_type=jnp.float32
            )
            * score_scale
        )
        return jnp.where(valid_four, scores, NEG_FILL)

    query_blocks = query.reshape(blocks, BLOCK, groups, GROUP_HEADS, HEAD_DIM)
    cot_blocks = cotangent.reshape(blocks, BLOCK, groups, GROUP_HEADS, HEAD_DIM)
    attended_parts = []
    totals = []
    for group_idx in range(groups):
        keys_group, vals_group = assemble(group_idx, random_kv)
        scores = score_block(query_blocks[:, :, group_idx], keys_group)
        row_max = jnp.max(scores, axis=-1, keepdims=True)
        weights = jnp.where(valid_four, jnp.exp(scores - row_max), 0.0)
        log_total = row_max + jnp.log(jnp.sum(weights, axis=-1, keepdims=True))
        probs_b = jnp.where(valid_four, jnp.exp(scores - log_total), 0.0).astype(jnp.bfloat16)
        attended_parts.append(
            jnp.einsum(
                "bhqk,bkhd->bqhd", probs_b, vals_group, preferred_element_type=jnp.float32
            ).astype(jnp.bfloat16)
        )
        totals.append(log_total)
    back_kv = unpack_blocks(
        lax.all_to_all(pack_blocks(), "ctx", split_axis=0, concat_axis=0, tiled=True)
    )
    win_acc = jnp.zeros((blocks + 2, BLOCK, 2, features), jnp.float32)
    glob_acc = jnp.zeros((GLOBALS, BLOCK, 2, features), jnp.float32)
    grad_query_parts = []
    random_terms = []
    for group_idx in range(groups):
        start_col = group_idx * group_width
        keys_group, vals_group = assemble(group_idx, back_kv)
        query_group = query_blocks[:, :, group_idx]
        cot_group = cot_blocks[:, :, group_idx]
        scores = score_block(query_group, keys_group)
        probs = jnp.where(valid_four, jnp.exp(scores - totals[group_idx]), 0.0)
        probs_b = probs.astype(jnp.bfloat16)
        row_dot = jnp.sum(
            cot_group.astype(jnp.float32) * attended_parts[group_idx].astype(jnp.float32), axis=-1
        )
        row_dot = jnp.transpose(row_dot, (0, 2, 1))[..., None]
        dprob = jnp.einsum(
            "bqhd,bkhd->bhqk", cot_group, vals_group, preferred_element_type=jnp.float32
        )
        dscore = (probs * (dprob - row_dot)).astype(jnp.bfloat16)
        grad_query_parts.append(
            (
                jnp.einsum(
                    "bhqk,bkhd->bqhd", dscore, keys_group, preferred_element_type=jnp.float32
                )
                * score_scale
            ).astype(jnp.bfloat16)
        )
        term_k = (
            jnp.einsum("bhqk,bqhd->bkhd", dscore, query_group, preferred_element_type=jnp.float32)
            * score_scale
        )
        term_v = jnp.einsum(
            "bhqk,bqhd->bkhd", probs_b, cot_group, preferred_element_type=jnp.float32
        )
        term_kv = jnp.stack((term_k, term_v), axis=2).reshape(
            blocks, key_kinds, BLOCK, 2, group_width
        )
        for offset in range(3):
            win_acc = win_acc.at[
                offset : offset + blocks, :, :, start_col : start_col + group_width
            ].add(term_kv[:, offset])
        glob_acc = glob_acc.at[:, :, :, start_col : start_col + group_width].add(
            jnp.sum(term_kv[:, 3 : 3 + GLOBALS], axis=0)
        )
        random_terms.append(term_kv[:, 3 + GLOBALS :].astype(jnp.bfloat16))
    random_flat = jnp.stack(random_terms, axis=1).reshape(
        blocks * pick_count, BLOCK, 2, group_width
    )
    grad_send = (
        jnp.zeros((device_count * slot_count, BLOCK, 2, group_width), jnp.bfloat16)
        .at[fetch_index]
        .set(random_flat)
    )
    grad_back = lax.all_to_all(
        grad_send.reshape(device_count, slot_count, BLOCK, 2, group_width),
        "ctx",
        split_axis=0,
        concat_axis=0,
        tiled=True,
    )
    grad_back = grad_back.reshape(device_count * slot_count, BLOCK, 2, group_width).astype(
        jnp.float32
    )
    grad_back = jnp.where(send_live[:, None, None, None], grad_back, 0.0)
    grad_owned = jnp.zeros((blocks, BLOCK, 2, groups, group_width), jnp.float32)
    grad_owned = grad_owned.at[send_block, :, :, send_group, :].add(grad_back)
    edge_sums = jnp.stack((win_acc[0], win_acc[blocks + 1]))
    edge_ext = padded_2(edge_sums, (("ctx", 0),), 1)
    glob_summed = lax.psum(glob_acc, "ctx")
    grad_total = win_acc[1 : blocks + 1] + grad_owned.reshape(blocks, BLOCK, 2, features)
    grad_total = grad_total.at[0].add(edge_ext[0]).at[blocks - 1].add(edge_ext[3])
    first_id = my_index * blocks + jnp.arange(blocks)
    for glob_index in range(GLOBALS):
        is_owner = global_ids[glob_index] == first_id
        grad_total = grad_total + jnp.where(
            is_owner[:, None, None, None], glob_summed[glob_index][None], 0.0
        )
    attended = jnp.stack(attended_parts, axis=2).reshape(tok_count, features)
    grad_query = jnp.stack(grad_query_parts, axis=2).reshape(tok_count, features)
    grad_key = grad_total[:, :, 0].reshape(tok_count, features).astype(jnp.bfloat16)
    grad_value = grad_total[:, :, 1].reshape(tok_count, features).astype(jnp.bfloat16)
    return (attended, grad_query, grad_key, grad_value)


def solution(mesh):
    return jax.shard_map(
        per_device,
        mesh=mesh,
        in_specs=(
            P(("groups", "ctx"), None),
            P(("groups", "ctx"), None),
            P(("groups", "ctx"), None),
            P(("groups", "ctx"), None),
            P("groups"),
            P("groups", None),
            P("groups", None),
        ),
        out_specs=(
            P(("groups", "ctx"), None),
            P(("groups", "ctx"), None),
            P(("groups", "ctx"), None),
            P(("groups", "ctx"), None),
        ),
        check_vma=False,
    )
```

profile of v0, /device:TPU:0, one launch (start us, length us, event | category | flops | bytes accessed | tf_op | source)
XLA Modules:
  0.0 543.7 jit_solution(3733437625669096891)
XLA Ops:
  7.2 1.4 stack.95
  8.7 1.4 stack.94
  12.2 2.8 gather_fusion
  15.0 4.5 broadcast_select_fusion
  19.4 7.6 %all-to-all-start = ((bf16[16,2,64,2,512]{4,2,3,1,0:T(8,128)(2,1)}), bf16[16,2,64,2,512]{4,2,3,1,0:T(8,128)(2,1)}, u32[]{:S(2)}, u32[]{:S(2)}) async-start(bf16[16,2,64,2,512]{4,2,3,1,0:T(8,128)(2,1)} %broadcast_select_fusion), calls=%async_computation | async-start | bytes 8388608 | tf_op jit(solution)/shard_map/all_to_all | solution.py:90
  33.9 3.0 collective-permute-start
  36.9 1.8 collective-permute-start.1
  39.4 1.8 reshape.639
  44.0 2.1 copy.242
  46.1 2.1 copy.241
  48.3 2.0 fusion.71
  50.3 130.1 %all-reduce.7.cloned.1.call-done = (bf16[1,64,2,1024]{3,1,2,0:T(8,128)(2,1)}, bf16[1,64,2,1024]{3,1,2,0:T(8,128)(2,1)}) async-done(((bf16[1,64,2,1024]{3,1,2,0:T(8,128)(2,1)}, bf16[1,64,2,1024]{3,1,2,0:T(8,128)(2,1)}), (bf16[1,64,2,1024]{3,1,2,0:T(8,128)(2,1)}, bf16[1,64,2,1024]{3,1,2,0:T(8,128)(2,1)})) %all-reduce.7.cloned.1.call-update) | async-done | bytes 524304 | tf_op jit(solution)/shard_map/psum | solution.py:31
  183.4 2.0 fusion.70
  185.5 1.5 broadcast_dynamic-update-slice_fusion
  187.0 2.9 gather_fusion.1
  190.0 1.9 fusion.29
  191.9 10.0 %copy.236 = bf16[4,8,64,2,512]{2,1,4,0,3:T(8,128)(2,1)} copy(bf16[4,8,64,2,512]{4,2,3,1,0:T(8,128)(2,1)} %get-tuple-element.138) | data formatting | bytes 8388608 | tf_op jit(solution)/shard_map/reshape | solution.py:121
  201.9 11.8 %reshape.691 = bf16[4,512,2,8,64]{1,4,3,0,2:T(8,128)(2,1)} reshape(bf16[4,8,64,2,512]{2,1,4,0,3:T(8,128)(2,1)} %copy.236) | data formatting | bytes 8388608 | tf_op jit(solution)/shard_map/reshape | solution.py:121
  213.7 10.0 %copy.234 = bf16[4,8,64,2,512]{2,1,4,0,3:T(8,128)(2,1)} copy(bf16[4,8,64,2,512]{4,2,3,1,0:T(8,128)(2,1)} %get-tuple-element.137) | data formatting | bytes 8388608 | tf_op jit(solution)/shard_map/reshape | solution.py:121
  223.7 11.8 %reshape.690 = bf16[4,512,2,8,64]{1,4,3,0,2:T(8,128)(2,1)} reshape(bf16[4,8,64,2,512]{2,1,4,0,3:T(8,128)(2,1)} %copy.234) | data formatting | bytes 8388608 | tf_op jit(solution)/shard_map/reshape | solution.py:121
  235.6 2.4 fusion.25
  238.5 1.4 bitcast_reduce_fusion.1
  239.9 2.3 fusion.9
  242.3 2.2 multiply_reduce_fusion
  244.6 3.2 convolution_bitcast_fusion
  247.8 2.2 multiply_reduce_fusion.1
  250.0 3.2 convolution_bitcast_fusion.1
  253.2 1.9 fusion
  255.1 2.6 fusion.1
  257.7 7.1 %reshape.688 = f32[4,8,64,1,512]{2,1,4,0,3:T(8,128)} reshape(f32[4,512,8,64]{1,3,2,0:T(8,128)} %convolution_bitcast_fusion) | data formatting | bytes 8388608 | tf_op jit(solution)/shard_map/stack | solution.py:188
  264.8 6.8 %copy.232 = f32[4,8,64,1,512]{4,2,1,0,3:T(8,128)} copy(f32[4,8,64,1,512]{2,1,4,0,3:T(8,128)} %reshape.688) | data formatting | bytes 8388608 | tf_op jit(solution)/shard_map/stack | solution.py:188
  271.6 2.7 multiply_bitcast_fusion
  274.3 7.1 %reshape.687 = f32[4,8,64,1,512]{2,1,4,0,3:T(8,128)} reshape(f32[4,512,8,64]{1,3,2,0:T(8,128)} %multiply_bitcast_fusion) | data formatting | bytes 8388608 | tf_op jit(solution)/shard_map/stack | solution.py:188
  281.4 6.8 %copy.231 = f32[4,8,64,1,512]{4,2,1,0,3:T(8,128)} copy(f32[4,8,64,1,512]{2,1,4,0,3:T(8,128)} %reshape.687) | data formatting | bytes 8388608 | tf_op jit(solution)/shard_map/stack | solution.py:188
  288.2 7.1 %reshape.686 = f32[4,8,64,1,512]{2,1,4,0,3:T(8,128)} reshape(f32[4,512,8,64]{1,3,2,0:T(8,128)} %convolution_bitcast_fusion.1) | data formatting | bytes 8388608 | tf_op jit(solution)/shard_map/stack | solution.py:188
  295.3 7.0 %copy.230 = f32[4,8,64,1,512]{4,2,1,0,3:T(8,128)} copy(f32[4,8,64,1,512]{2,1,4,0,3:T(8,128)} %reshape.686) | data formatting | bytes 8388608 | tf_op jit(solution)/shard_map/stack | solution.py:188
  302.2 2.7 multiply_bitcast_fusion.1
  305.0 7.1 %reshape.685 = f32[4,8,64,1,512]{2,1,4,0,3:T(8,128)} reshape(f32[4,512,8,64]{1,3,2,0:T(8,128)} %multiply_bitcast_fusion.1) | data formatting | bytes 8388608 | tf_op jit(solution)/shard_map/stack | solution.py:188
  312.0 6.9 %copy.229 = f32[4,8,64,1,512]{4,2,1,0,3:T(8,128)} copy(f32[4,8,64,1,512]{2,1,4,0,3:T(8,128)} %reshape.685) | data formatting | bytes 8388608 | tf_op jit(solution)/shard_map/stack | solution.py:188
  318.9 2.3 fusion.27
  324.1 2.5 broadcast_in_dim.190
  326.5 7.5 %scatter_fusion = bf16[32,64,2,512]{3,1,2,0:T(8,128)(2,1)} fusion(bf16[32,64,2,512]{3,1,2,0:T(8,128)(2,1)} %broadcast_in_dim.190, s32[24]{0:T(128)S(1)} %fusion.86, bf16[24,64,2,512]{3,1,2,0:T(8,128)(2,1)S(1)} %bitcast.294), kind=kCustom, calls=%fused_computation.2 | custom fusion | bytes 9437280 | tf_op jit(solution)/shard_map/scatter | solution.py:205
  334.1 5.4 all-to-all-start.1
  339.6 1.3 fusion.87
  341.6 1.9 and_reduce_fusion
  345.0 1.5 reshape.641
  346.5 3.1 fusion.36
  349.9 2.3 fusion.37
  353.5 1.5 reshape.643
  355.0 1.5 fusion.50
  357.5 1.5 copy-done.5
  359.6 1.9 copy-done
  362.7 3.1 add_select_fusion
  365.9 5.7 %scatter-add.41 = f32[6,64,2,1024]{3,1,0,2:T(8,128)S(1)} dynamic-update-slice(f32[6,64,2,1024]{3,1,0,2:T(8,128)S(1)} %fusion.58, f32[4,64,2,512]{3,1,0,2:T(8,128)} %add_select_fusion, s32[]{:T(128)} %bitcast.48, s32[]{:T(128)} %constant.374.clone.1, s32[]{:T(128)} %constant.374.clone.1, s32[]{:T(128)} %bitcast.49) | dynamic-update-slice | bytes 2097156 | tf_op jit(solution)/shard_map/scatter-add | solution.py:194
  371.6 2.0 fusion.18
  377.0 1.7 fusion.44
  382.2 3.1 collective-permute-start.2
  386.6 115.3 %all-reduce.5.cloned.1.call-done = f32[2,64,2,1024]{3,1,0,2:T(8,128)} async-done(((f32[2,64,2,1024]{3,1,0,2:T(8,128)}), f32[2,64,2,1024]{3,1,0,2:T(8,128)}) %all-reduce.5.cloned.1.call-update) | async-done | bytes 1048592 | tf_op jit(solution)/shard_map/psum | solution.py:222
  501.9 2.3 slice_bitcast_fusion.31
  504.2 6.9 %convert_select_fusion = f32[32,64,2,512]{3,1,2,0:T(8,128)} fusion(bf16[16,2,64,2,512]{4,2,3,1,0:T(8,128)(2,1)} %all-to-all-done.1, pred[32]{0:T(512)(128)(4,1)S(1)} %gt.20), kind=kLoop, calls=%fused_computation.20 | loop fusion | flops 4194304 | bytes 12582944 | tf_op jit(solution)/shard_map/jit(_where)/select_n | solution.py:217
  511.3 12.2 %scatter_fusion.1 = f32[4,64,2,2,512]{4,1,3,2,0:T(8,128)S(1)} fusion(f32[4,64,2,2,512]{4,1,3,2,0:T(8,128)S(1)} %broadcast_in_dim.188, s32[32]{0:T(128)S(1)} %get-tuple-element.133, f32[32,64,2,512]{3,1,2,0:T(8,128)} %convert_select_fusion), kind=kCustom, calls=%fused_computation.3 | custom fusion | flops 2097152 | bytes 25166080 | tf_op jit(solution)/shard_map/scatter-add | solution.py:219
  523.5 2.9 copy.233
  526.4 4.2 reshape.689
  530.6 2.1 slice_add_fusion
  (138 shorter events, 32.7 us)
Async XLA Ops:
  7.2 3.1 copy-start.28
  7.2 4.0 copy-start.29
  19.4 7.7 %copy-start.30 = (s32[2]{0:T(128)S(1)}, s32[2]{0:T(128)}, u32[]{:S(2)}) copy-start(s32[2]{0:T(128)} %param.31) | copy-start | bytes 28
  19.4 13.5 %copy-start.12 = (bf16[256,1024]{1,0:T(8,128)(2,1)S(1)}, bf16[256,1024]{1,0:T(8,128)(2,1)}, u32[]{:S(2)}) copy-start(bf16[256,1024]{1,0:T(8,128)(2,1)} %param.28) | copy-start | bytes 1572868
  19.4 13.5 %copy-start.13 = (bf16[256,1024]{1,0:T(8,128)(2,1)S(1)}, bf16[256,1024]{1,0:T(8,128)(2,1)}, u32[]{:S(2)}) copy-start(bf16[256,1024]{1,0:T(8,128)(2,1)} %param.29) | copy-start | bytes 1572868
  19.4 19.3 %copy-start.25 = (bf16[256,1024]{1,0:T(8,128)(2,1)S(1)}, bf16[256,1024]{1,0:T(8,128)(2,1)}, u32[]{:S(2)}) copy-start(bf16[256,1024]{1,0:T(8,128)(2,1)} %param.30) | copy-start | bytes 1572868
  19.4 167.6 %all-to-all-start = ((bf16[16,2,64,2,512]{4,2,3,1,0:T(8,128)(2,1)}), bf16[16,2,64,2,512]{4,2,3,1,0:T(8,128)(2,1)}, u32[]{:S(2)}, u32[]{:S(2)}) async-start(bf16[16,2,64,2,512]{4,2,3,1,0:T(8,128)(2,1)} %broadcast_select_fusion), calls=%async_computation | async-start | bytes 8388608 | tf_op jit(solution)/shard_map/all_to_all | solution.py:90
  27.1 153.3 %all-reduce.7.cloned.1.call-start = ((), (), s32[]{:S(2)}) async-start(), calls=%async_computation.3 | async-start | bytes 1048576 | tf_op jit(solution)/shard_map/psum | solution.py:31
  33.9 14.4 %collective-permute-start = (bf16[1,64,2,1024]{3,1,2,0:T(8,128)(2,1)}, bf16[1,64,2,1024]{3,1,2,0:T(8,128)(2,1)}, u32[]{:S(2)}, u32[]{:S(2)}) collective-permute-start(bf16[1,64,2,1024]{3,1,2,0:T(8,128)(2,1)} %get-tuple-element.154), channel_id=1, source_target_pairs={{0,1},{1,2},{2,3},{3,4},{4,5},{5,6},{6,7},{7,8},{8,9},{9,10},{10,1... | collective-permute-start | bytes 786440 | tf_op jit(solution)/shard_map/ppermute | solution.py:21
  36.9 146.6 %collective-permute-start.1 = (bf16[1,64,2,1024]{3,1,2,0:T(8,128)(2,1)S(1)}, bf16[1,64,2,1024]{3,1,2,0:T(8,128)(2,1)}, u32[]{:S(2)}, u32[]{:S(2)}) collective-permute-start(bf16[1,64,2,1024]{3,1,2,0:T(8,128)(2,1)S(1)} %get-tuple-element.155), channel_id=1, source_target_pairs={{1,0},{2,1},{3,2},{4,3},{5,4},{6,5},{7,6},{8,7},{9,8},{10,9},{11,1... | collective-permute-start | bytes 786440 | tf_op jit(solution)/shard_map/ppermute | solution.py:24
  223.7 11.8 %copy-start.18 = (bf16[4,64,1,8,64]{4,3,2,1,0:T(8,128)(2,1)S(1)}, bf16[4,64,1,8,64]{4,3,2,1,0:T(8,128)(2,1)}, u32[]{:S(2)}) copy-start(bf16[4,64,1,8,64]{4,3,2,1,0:T(8,128)(2,1)} %get-tuple-element.150) | copy-start | bytes 786436
  235.6 2.8 copy-start.15
  235.6 2.9 copy-start.17
  239.9 2.4 copy-start.14
  239.9 2.4 copy-start.20
  244.6 3.2 copy-start.19
  255.1 16.5 %copy-start.21 = (bf16[4,8,64,512]{3,2,1,0:T(8,128)(2,1)}, bf16[4,8,64,512]{3,2,1,0:T(8,128)(2,1)S(1)}, u32[]{:S(2)}) copy-start(bf16[4,8,64,512]{3,2,1,0:T(8,128)(2,1)S(1)} %fusion) | copy-start | bytes 6291460
  295.3 7.0 %copy-start.22 = (bf16[4,8,64,512]{3,2,1,0:T(8,128)(2,1)S(1)}, bf16[4,8,64,512]{3,2,1,0:T(8,128)(2,1)}, u32[]{:S(2)}) copy-start(bf16[4,8,64,512]{3,2,1,0:T(8,128)(2,1)} %fusion.1) | copy-start | bytes 6291460
  318.9 3.1 copy-start.4
  318.9 4.4 copy-start.7
  334.1 7.5 %copy-start.31 = (s32[4]{0:T(128)S(1)}, s32[4]{0:T(128)}, u32[]{:S(2)}) copy-start(s32[4]{0:T(128)} %constant.391.clone.1) | copy-start | bytes 52
  334.1 9.4 %copy-start.26 = (bf16[4,8,64,64]{3,2,1,0:T(8,128)(2,1)S(1)}, bf16[4,8,64,64]{3,2,1,0:T(8,128)(2,1)}, u32[]{:S(2)}) copy-start(bf16[4,8,64,64]{3,2,1,0:T(8,128)(2,1)} %get-tuple-element.165) | copy-start | bytes 786436
  334.1 9.4 %copy-start.27 = (bf16[4,8,64,64]{3,2,1,0:T(8,128)(2,1)S(1)}, bf16[4,8,64,64]{3,2,1,0:T(8,128)(2,1)}, u32[]{:S(2)}) copy-start(bf16[4,8,64,64]{3,2,1,0:T(8,128)(2,1)} %get-tuple-element.167) | copy-start | bytes 786436
  334.1 170.1 %all-to-all-start.1 = ((bf16[16,2,64,2,512]{4,2,3,1,0:T(8,128)(2,1)}), bf16[16,2,64,2,512]{4,2,3,1,0:T(8,128)(2,1)}, u32[]{:S(2)}, u32[]{:S(2)}) async-start(bf16[16,2,64,2,512]{4,2,3,1,0:T(8,128)(2,1)} %bitcast.283), calls=%async_computation.1 | async-start | bytes 8388608 | tf_op jit(solution)/shard_map/all_to_all | solution.py:207
  339.5 162.4 %all-reduce.5.cloned.1.call-start = ((), (), s32[]{:S(2)}) async-start(), calls=%async_computation.2 | async-start | bytes 2097152 | tf_op jit(solution)/shard_map/psum | solution.py:222
  346.5 3.4 copy-start.16
  355.0 2.5 copy-start.8
  356.4 2.6 copy-start.5
  359.3 2.2 copy-start
  359.3 3.5 copy-start.2
  371.6 2.8 copy-start.6
  371.6 4.1 copy-start.9
  377.0 2.5 copy-start.1
  377.0 3.8 copy-start.3
  381.1 130.0 %copy-start.10 = (f32[6,64,2,1024]{3,1,0,2:T(8,128)}, f32[6,64,2,1024]{3,1,0,2:T(8,128)S(1)}, u32[]{:S(2)}) copy-start(f32[6,64,2,1024]{3,1,0,2:T(8,128)S(1)} %fusion.48) | copy-start | bytes 9437188
  382.2 150.5 %collective-permute-start.2 = (f32[1,64,2,1024]{3,1,0,2:T(8,128)}, f32[1,64,2,1024]{3,1,0,2:T(8,128)}, u32[]{:S(2)}, u32[]{:S(2)}) collective-permute-start(f32[1,64,2,1024]{3,1,0,2:T(8,128)} %get-tuple-element.136), channel_id=1, source_target_pairs={{0,1},{1,2},{2,3},{3,4},{4,5},{5,6},{6,7},{7,8},{8,9},{9,10},{10,1... | collective-permute-start | bytes 1572872 | tf_op jit(solution)/shard_map/ppermute | solution.py:21
  385.3 148.6 %collective-permute-start.3 = (f32[1,64,2,1024]{3,1,0,2:T(8,128)}, f32[1,64,2,1024]{3,1,0,2:T(8,128)}, u32[]{:S(2)}, u32[]{:S(2)}) collective-permute-start(f32[1,64,2,1024]{3,1,0,2:T(8,128)} %get-tuple-element.135), channel_id=1, source_target_pairs={{1,0},{2,1},{3,2},{4,3},{5,4},{6,5},{7,6},{8,7},{9,8},{10,9},{11,1... | collective-permute-start | bytes 1572872 | tf_op jit(solution)/shard_map/ppermute | solution.py:24
  526.4 4.2 copy-start.11
  530.6 4.5 copy-start.23
  530.6 4.5 copy-start.24
Sparse Core Ops, SparseCore 0:
  38.8 141.5 all-reduce.6
  377.1 124.7 all-reduce.4
where the time goes:
time: 550 us; the launch traced here: 544 us
  waiting for transfers between devices  245 us (45%)
  local copies, waits for them, and re-layouts  171 us (31%)
  other arithmetic  54.9 us (10%)
  matrix products  30.1 us (5%)
  starting transfers between devices  22.2 us (4%)
  between operations  20.1 us (4%)
    psum x1, waiting for transfers between devices, broadcast(): return lax.psum(jnp.where(mine, array, jnp.zeros_like(array)), axis)  130 us
    psum x1, waiting for transfers between devices, per_device(): glob_summed = lax.psum(glob_acc, 'ctx')  115 us
    another operation x8, local copies, waits for them, and re-layouts, per_device(): jnp.stack((term_k, term_v), axis=2)  55.7 us
    reshape x4, local copies, waits for them, and re-layouts, assemble(): joined = joined.reshape(blocks, key_span, 2, GROUP_HEADS, HEAD_DIM)  43.7 us
    unnamed x70, local copies, waits for them, and re-layouts  19.5 us
    scatter-add x1, other arithmetic, per_device(): grad_owned = grad_owned.at[send_block, :, :, send_group, :].add(grad_back)  12.2 us
  transfers between devices with their start and end apart: 8, of which 2 were waited for; matrix products, arithmetic and copies ran while one was open for 15% of the time, Pallas kernels for 0%

commit v1 on v0

v1 whole, which is shorter than its diff:
```python
import functools

import jax
import jax.numpy as jnp
from jax import lax
from jax.experimental import pallas as pl
from jax.experimental.pallas import tpu as pltpu
from jax.sharding import PartitionSpec as P

HEAD_DIM = 64
GROUP_HEADS = 8
BLOCK = 64
GLOBALS = 2
ROUNDS = 3
KINDS = 3 + GLOBALS + ROUNDS
PAIR = 2 * HEAD_DIM
NEG_FILL = -1e30
SCALE = HEAD_DIM ** (-0.5)
UNROLL = 2


def pack_kernel(q_ref, k_ref, v_ref, d_ref, qd_ref, kv_ref):
    heads = kv_ref.shape[0]
    for pair in range(heads // 2):
        cols = slice(pair * PAIR, (pair + 1) * PAIR)
        for left_ref, right_ref, out_ref in ((q_ref, d_ref, qd_ref), (k_ref, v_ref, kv_ref)):
            left = left_ref[:, cols]
            right = right_ref[:, cols]
            out_ref[2 * pair] = jnp.concatenate([left[:, :HEAD_DIM], right[:, :HEAD_DIM]], axis=1)
            out_ref[2 * pair + 1] = jnp.concatenate(
                [left[:, HEAD_DIM:], right[:, HEAD_DIM:]], axis=1
            )


def unpack_kernel(qo_ref, kv_ref, att_ref, gq_ref, gk_ref, gv_ref):
    heads = kv_ref.shape[0]
    for pair in range(heads // 2):
        cols = slice(pair * PAIR, (pair + 1) * PAIR)
        for in_ref, left_ref, right_ref in ((qo_ref, gq_ref, att_ref), (kv_ref, gk_ref, gv_ref)):
            even = in_ref[2 * pair]
            odd = in_ref[2 * pair + 1]
            left_ref[:, cols] = jnp.concatenate([even[:, :HEAD_DIM], odd[:, :HEAD_DIM]], axis=1)
            right_ref[:, cols] = jnp.concatenate([even[:, HEAD_DIM:], odd[:, HEAD_DIM:]], axis=1)


def attend_kernel(query_blocks, ids_ref, edge_ref, qd_ref, kv_ref, qo_ref, gkv_ref, acc_ref):
    acc_ref[...] = jnp.zeros_like(acc_ref)
    lane = lax.broadcasted_iota(jnp.int32, (BLOCK, PAIR), 1)
    low = lane < HEAD_DIM
    row_lane = lax.broadcasted_iota(jnp.int32, (1, PAIR), 1)
    contract_last = (((1,), (1,)), ((), ()))
    contract_first = (((0,), (0,)), ((), ()))

    def front(index):
        rows = pl.ds(pl.multiple_of(index * BLOCK, BLOCK), BLOCK)
        qd = qd_ref[rows, :]
        spots = [
            pl.ds(pl.multiple_of(ids_ref[index * KINDS + kind] * BLOCK, BLOCK), BLOCK)
            for kind in range(KINDS)
        ]
        kv = jnp.concatenate([kv_ref[spot, :] for spot in spots], axis=0)
        zero = jnp.zeros_like(qd)
        diag = jnp.concatenate(
            [jnp.where(low, qd * jnp.bfloat16(SCALE), zero), jnp.where(low, zero, qd)], axis=0
        )
        both = lax.dot_general(diag, kv, contract_last, preferred_element_type=jnp.float32)
        scores = both[:BLOCK]
        dprob = both[BLOCK:]
        no_left = edge_ref[2 * index] == 1
        no_right = edge_ref[2 * index + 1] == 1
        bias = jnp.where(
            row_lane < BLOCK,
            jnp.where(no_left, NEG_FILL, 0.0),
            jnp.where(no_right, NEG_FILL, 0.0),
        ).astype(jnp.float32)
        scores = jnp.concatenate([scores[:, :PAIR] + bias, scores[:, PAIR:]], axis=1)
        row_max = jnp.max(scores, axis=1, keepdims=True)
        weights = jnp.exp(scores - row_max)
        probs = weights * (1.0 / jnp.sum(weights, axis=1, keepdims=True))
        probs_b = probs.astype(jnp.bfloat16)
        attended = jnp.dot(probs_b, kv, preferred_element_type=jnp.float32).astype(jnp.bfloat16)
        row_dot = jnp.sum(
            jnp.where(low, 0.0, qd.astype(jnp.float32) * attended.astype(jnp.float32)),
            axis=1,
            keepdims=True,
        )
        dscore = (probs * (dprob - row_dot)).astype(jnp.bfloat16)
        grad_q = jnp.dot(dscore, kv, preferred_element_type=jnp.float32) * SCALE
        qo_ref[rows, :] = jnp.where(low, grad_q.astype(jnp.bfloat16), attended)
        terms = lax.dot_general(
            jnp.concatenate([dscore, probs_b], axis=0),
            diag,
            contract_first,
            preferred_element_type=jnp.float32,
        )
        return spots, terms

    def step(number, carry):
        done = [front(number * UNROLL + part) for part in range(UNROLL)]
        for spots, terms in done:
            for kind in range(KINDS):
                acc_ref[spots[kind], :] += terms[kind * BLOCK : (kind + 1) * BLOCK]
        return carry

    lax.fori_loop(0, query_blocks // UNROLL, step, 0)
    gkv_ref[...] = acc_ref[...].astype(gkv_ref.dtype)


VMEM = pl.BlockSpec(memory_space=pltpu.VMEM)
SMEM = pl.BlockSpec(memory_space=pltpu.SMEM)


def per_device(query, key, value, cotangent, global_ids, rand_owner, rand_local):
    tokens, features = query.shape
    blocks = tokens // BLOCK
    heads = features // HEAD_DIM
    groups = heads // GROUP_HEADS
    count = lax.axis_size("ctx")
    me = lax.axis_index("ctx")
    shares = count // heads
    own_blocks = blocks // shares
    own_tokens = own_blocks * BLOCK
    all_blocks = count * blocks
    half = jax.ShapeDtypeStruct((heads, tokens, PAIR), jnp.bfloat16)
    qd, kv = pl.pallas_call(
        pack_kernel,
        out_shape=(half, half),
        in_specs=[VMEM] * 4,
        out_specs=(VMEM, VMEM),
        name="pack",
    )(query, key, value, cotangent)
    qd_send = qd.reshape(count, own_tokens, PAIR)
    kv_send = jnp.broadcast_to(kv[:, None], (heads, shares, tokens, PAIR)).reshape(
        count, tokens, PAIR
    )
    exchange = functools.partial(
        lax.all_to_all, axis_name="ctx", split_axis=0, concat_axis=0, tiled=True
    )
    kv_all = exchange(kv_send).reshape(count * tokens, PAIR)
    qd_all = exchange(qd_send).reshape(count * own_tokens, PAIR)

    my_group = me // shares // GROUP_HEADS
    share = me % shares
    picked = (rand_owner * blocks + rand_local).reshape(all_blocks, groups, ROUNDS)
    picked = lax.dynamic_index_in_dim(picked, my_group, 1, keepdims=False)
    here = jnp.arange(all_blocks, dtype=jnp.int32)
    table = jnp.concatenate(
        [
            jnp.maximum(here - 1, 0)[:, None],
            jnp.minimum(here + 1, all_blocks - 1)[:, None],
            here[:, None],
            jnp.broadcast_to(global_ids[None, :], (all_blocks, GLOBALS)),
            picked,
        ],
        axis=1,
    ).astype(jnp.int32)
    edges = jnp.stack([here == 0, here == all_blocks - 1], axis=1).astype(jnp.int32)

    def mine(array):
        split = array.reshape(count, shares, own_blocks, array.shape[1])
        return lax.dynamic_index_in_dim(split, share, 1, keepdims=False).reshape(-1)

    qo_all, gkv_all = pl.pallas_call(
        functools.partial(attend_kernel, count * own_blocks),
        out_shape=(
            jax.ShapeDtypeStruct((count * own_tokens, PAIR), jnp.bfloat16),
            jax.ShapeDtypeStruct((count * tokens, PAIR), jnp.bfloat16),
        ),
        in_specs=[SMEM, SMEM, VMEM, VMEM],
        out_specs=(VMEM, VMEM),
        scratch_shapes=[pltpu.VMEM((count * tokens, PAIR), jnp.float32)],
        compiler_params=pltpu.CompilerParams(vmem_limit_bytes=40 * 1024 * 1024),
        name="attend",
    )(mine(table), mine(edges), qd_all, kv_all)
    qo = exchange(qo_all.reshape(count, own_tokens, PAIR)).reshape(heads, tokens, PAIR)
    gkv = exchange(gkv_all.reshape(count, tokens, PAIR)).reshape(heads, shares, tokens, PAIR)
    if shares == 1:
        gkv = gkv[:, 0]
    else:
        gkv = jnp.sum(gkv.astype(jnp.float32), axis=1).astype(jnp.bfloat16)
    flat = jax.ShapeDtypeStruct((tokens, features), jnp.bfloat16)
    return pl.pallas_call(
        unpack_kernel,
        out_shape=(flat,) * 4,
        in_specs=[VMEM] * 2,
        out_specs=(VMEM,) * 4,
        name="unpack",
    )(qo, gkv)


def solution(mesh):
    rows = P(("groups", "ctx"), None)
    return jax.shard_map(
        per_device,
        mesh=mesh,
        in_specs=(rows, rows, rows, rows, P("groups"), P("groups", None), P("groups", None)),
        out_specs=(rows,) * 4,
        check_vma=False,
    )
```

time: 550 us -> 177 us (0.32)
  waiting for transfers between devices: 245 us -> 20.9 us
  local copies, waits for them, and re-layouts: 171 us -> 1.85 us
  blocking collectives: 0 us -> 93.1 us
  other arithmetic: 54.9 us -> 0.02 us
  Pallas kernels: 0 us -> 54.4 us
  matrix products: 30.1 us -> 0 us
  between operations: 20.1 us -> 0.72 us
  starting transfers between devices: 22.2 us -> 5.03 us
    psum x2 -> x0, waiting for transfers between devices: 245 us -> none  [the longest x1 130 us: broadcast(): return lax.psum(jnp.where(mine, array, jnp.zeros_like(array)), axis)]
    all_to_all x0 -> x3, blocking collectives: none -> 93.1 us  [the longest x1 32.1 us: per_device(): qd_all = exchange(qd_send).reshape(count * own_tokens, PAIR)]
    another operation x19 -> x0, local copies, waits for them, and re-layouts: 62.8 us -> none  [the longest x8 55.7 us: per_device(): jnp.stack((term_k, term_v), axis=2)]
    reshape x14 -> x2, local copies, waits for them, and re-layouts: 56.6 us -> 0.1 us  [the longest x1 0.09 us: mine(): return lax.dynamic_index_in_dim(split, share, 1, keepdims=False).reshape(-1)]
    pallas_call x0 -> x3, Pallas kernels: none -> 54.4 us  [the longest x1 47.4 us: per_device(): pl.pallas_call(functools.partial(attend_kernel, count * own_blocks), out_...]
    dot_general x12 -> x0, matrix products: 30.1 us -> none  [the longest x2 6.39 us: per_device(): jnp.einsum('bhqk,bqhd->bkhd', probs_b, cot_group, preferred_element_type=...]
    all_to_all x2 -> x1, waiting for transfers between devices: 0.01 us -> 20.9 us  [per_device(): kv_all = exchange(kv_send).reshape(count * tokens, PAIR)]
    unnamed x70 -> x6, local copies, waits for them, and re-layouts: 19.5 us -> 1.32 us
  transfers between devices with their start and end apart: 8 -> 1, of which waited for: 2 -> 1; matrix products, arithmetic and copies ran while one was open for 15% -> 0% of each run, Pallas kernels for 0% -> 0%
where the time goes in v1:
time: 177 us; the launch traced here: 176 us
  blocking collectives  93.1 us (53%)
  Pallas kernels  54.4 us (31%)
  waiting for transfers between devices  20.9 us (12%)
  starting transfers between devices  5.03 us (3%)
  local copies, waits for them, and re-layouts  1.85 us (1%)
    pallas_call x1, Pallas kernels, per_device(): pl.pallas_call(functools.partial(attend_kernel, count * own_blocks), out_...  47.4 us
    all_to_all x1, blocking collectives, per_device(): qd_all = exchange(qd_send).reshape(count * own_tokens, PAIR)  32.1 us
    all_to_all x1, blocking collectives, per_device(): exchange(gkv_all.reshape(count, tokens, PAIR))  31.4 us
    all_to_all x1, blocking collectives, per_device(): exchange(qo_all.reshape(count, own_tokens, PAIR))  29.6 us
    all_to_all x1, waiting for transfers between devices, per_device(): kv_all = exchange(kv_send).reshape(count * tokens, PAIR)  20.9 us
    all_to_all x1, starting transfers between devices, per_device(): kv_all = exchange(kv_send).reshape(count * tokens, PAIR)  5.03 us
  transfers between devices with their start and end apart: 1, of which 1 were waited for; matrix products, arithmetic and copies ran while one was open for 0% of the time, Pallas kernels for 0%

profile of v1, /device:TPU:0, one launch (start us, length us, event | category | flops | bytes accessed | tf_op | source)
XLA Modules:
  0.0 176.0 jit_solution(931073398018772427)
XLA Ops:
  0.6 3.4 %pack.1 = (bf16[16,256,128]{2,1,0:T(8,128)(2,1)}, bf16[16,256,128]{2,1,0:T(8,128)(2,1)}) custom-call(bf16[256,1024]{1,0:T(8,128)(2,1)} %q_ref.1, bf16[256,1024]{1,0:T(8,128)(2,1)} %k_ref.1, bf16[256,1024]{1,0:T(8,128)(2,1)} %v_ref.1, bf16[256,1024]{1,0:T(8,128)(2,1)} %d_ref.1), custom_call_target="tpu_custom_call" | custom-call | tf_op jit(solution)/shard_map/pack/pallas_call | solution.py:125
  4.1 32.1 %all_to_all.20 = bf16[16,256,128]{2,1,0:T(8,128)(2,1)S(1)} all-to-all(bf16[16,256,128]{2,1,0:T(8,128)(2,1)} %get-tuple-element.8), channel_id=1, replica_groups=mesh['groups'=2,'ctx'=16] {'ctx'}, dimensions={0} | all-to-all | bytes 2097152 | tf_op jit(solution)/shard_map/all_to_all | solution.py:140
  36.2 5.0 %all-to-all-start.1 = ((bf16[16,256,128]{2,1,0:T(8,128)(2,1)}), bf16[16,256,128]{2,1,0:T(8,128)(2,1)S(1)}, u32[]{:S(2)}, u32[]{:S(2)}) async-start(bf16[16,256,128]{2,1,0:T(8,128)(2,1)} %get-tuple-element.9), calls=%async_computation.1 | async-start | bytes 2097152 | tf_op jit(solution)/shard_map/all_to_all | solution.py:139
  41.2 0.0 copy-start.1
  41.2 0.0 copy-start
  41.2 0.7 copy-done.1
  41.9 0.0 copy-done
  41.9 0.0 copy-start.2
  42.0 0.6 copy-done.2
  42.6 0.1 broadcast_in_dim.2
  42.7 0.1 copy.13
  42.8 0.1 reshape.72.ids_ref
  42.9 0.1 copy.14
  43.0 0.1 reshape.77.edge_ref
  43.1 20.9 %all-to-all-done.1 = bf16[16,256,128]{2,1,0:T(8,128)(2,1)S(1)} async-done(((bf16[16,256,128]{2,1,0:T(8,128)(2,1)}), bf16[16,256,128]{2,1,0:T(8,128)(2,1)S(1)}, u32[]{:S(2)}, u32[]{:S(2)}) %all-to-all-start.1) | async-done | bytes 1048608 | tf_op jit(solution)/shard_map/all_to_all | solution.py:139
  64.1 47.4 %attend.1 = (bf16[4096,128]{1,0:T(8,128)(2,1)S(1)}, bf16[4096,128]{1,0:T(8,128)(2,1)S(1)}) custom-call(s32[512]{0:T(512)S(1)} %reshape.72.ids_ref, s32[128]{0:T(128)S(1)} %reshape.77.edge_ref, bf16[4096,128]{1,0:T(8,128)(2,1)S(1)} %bitcast.8, bf16[4096,128]{1,0:T(8,128)(2,1)S(1)} %bitcast.9), custom_call_target="tpu_custom_call" | custom-call | tf_op jit(solution)/shard_map/attend/pallas_call | solution.py:163
  111.5 31.4 %all_to_all.21.kv_ref = bf16[16,256,128]{2,1,0:T(8,128)(2,1)} all-to-all(bf16[16,256,128]{2,1,0:T(8,128)(2,1)S(1)} %bitcast.11), channel_id=1, replica_groups=mesh['groups'=2,'ctx'=16] {'ctx'}, dimensions={0} | all-to-all | bytes 2097152 | tf_op jit(solution)/shard_map/all_to_all | solution.py:176
  142.9 29.6 %all_to_all.22.qo_ref = bf16[16,256,128]{2,1,0:T(8,128)(2,1)} all-to-all(bf16[16,256,128]{2,1,0:T(8,128)(2,1)S(1)} %bitcast.10), channel_id=1, replica_groups=mesh['groups'=2,'ctx'=16] {'ctx'}, dimensions={0} | all-to-all | bytes 2097152 | tf_op jit(solution)/shard_map/all_to_all | solution.py:175
  172.5 3.5 %unpack.1 = (bf16[256,1024]{1,0:T(8,128)(2,1)}, bf16[256,1024]{1,0:T(8,128)(2,1)}, bf16[256,1024]{1,0:T(8,128)(2,1)}, bf16[256,1024]{1,0:T(8,128)(2,1)}) custom-call(bf16[16,256,128]{2,1,0:T(8,128)(2,1)} %all_to_all.22.qo_ref, bf16[16,256,128]{2,1,0:T(8,128)(2,1)} %all_to_all.21.kv_ref), custom_call_target="tpu_custom_call" | custom-call | tf_op jit(solution)/shard_map/unpack/pallas_call | solution.py:182
  (8 shorter events, 0.1 us)
Async XLA Ops:
  36.2 27.9 %all-to-all-start.1 = ((bf16[16,256,128]{2,1,0:T(8,128)(2,1)}), bf16[16,256,128]{2,1,0:T(8,128)(2,1)S(1)}, u32[]{:S(2)}, u32[]{:S(2)}) async-start(bf16[16,256,128]{2,1,0:T(8,128)(2,1)} %get-tuple-element.9), calls=%async_computation.1 | async-start | bytes 2097152 | tf_op jit(solution)/shard_map/all_to_all | solution.py:139
  41.2 0.7 copy-start.1
  41.2 0.7 copy-start
  41.9 0.7 copy-start.2

commit v2 on v1

v2 whole, which is shorter than its diff:
```python
import functools

import jax
import jax.numpy as jnp
from jax import lax
from jax.experimental import pallas as pl
from jax.experimental.pallas import tpu as pltpu
from jax.sharding import PartitionSpec as P

HEAD_DIM = 64
GROUP_HEADS = 8
BLOCK = 64
GLOBALS = 2
ROUNDS = 3
KINDS = 3 + GLOBALS + ROUNDS
PAIR = 2 * HEAD_DIM
NEG_FILL = -1e30
SCALE = HEAD_DIM ** (-0.5)
MESH = pl.DeviceIdType.MESH


def lanes_joined(left, right):
    return jnp.concatenate([left, right], axis=1)


def greet(me, count):
    barrier = pltpu.get_barrier_semaphore()
    for step in range(1, count):
        peer = lax.rem(me + step, count)
        pl.semaphore_signal(barrier, inc=1, device_id={"ctx": peer}, device_id_type=MESH)
    return barrier


def attend_kernel(
    count,
    shares,
    ids_ref,
    q_ref,
    k_ref,
    v_ref,
    d_ref,
    qo_got,
    acc_ref,
    glob_ref,
    rand_ref,
    kv_pack,
    qd_pack,
    kv_all,
    qd_all,
    qo_put,
    kv_out,
    kv_in,
    qd_out,
    qd_in,
    qo_out,
    qo_in,
):
    me = lax.axis_index("ctx")
    heads, tokens = kv_pack.shape[:2]
    blocks = tokens // BLOCK
    own_tokens = tokens // shares
    own_blocks = own_tokens // BLOCK
    all_blocks = count * blocks
    my_share = lax.rem(me, shares)

    barrier = greet(me, count)
    for pair in range(heads // 2):
        cols = slice(pair * PAIR, (pair + 1) * PAIR)
        for left_ref, right_ref, out_ref in ((k_ref, v_ref, kv_pack), (q_ref, d_ref, qd_pack)):
            left = left_ref[:, cols]
            right = right_ref[:, cols]
            out_ref[2 * pair] = lanes_joined(left[:, :HEAD_DIM], right[:, :HEAD_DIM])
            out_ref[2 * pair + 1] = lanes_joined(left[:, HEAD_DIM:], right[:, HEAD_DIM:])
    my_head = me // shares
    my_rows = pl.ds(pl.multiple_of(my_share * own_tokens, own_tokens), own_tokens)
    for part in range(blocks):
        kv_all[me * blocks + part] = kv_pack[my_head, part * BLOCK : (part + 1) * BLOCK]
    qd_all[me] = qd_pack[my_head, my_rows, :]
    acc_ref[...] = jnp.zeros_like(acc_ref)
    glob_ref[...] = jnp.zeros_like(glob_ref)
    pl.semaphore_wait(barrier, count - 1)

    def kv_copy(dest, came):
        return pltpu.make_async_remote_copy(
            src_ref=kv_pack.at[dest // shares].reshape(blocks, BLOCK, PAIR),
            dst_ref=kv_all.at[pl.ds(came * blocks, blocks)],
            send_sem=kv_out.at[dest],
            recv_sem=kv_in.at[came],
            device_id={"ctx": dest},
            device_id_type=MESH,
        )

    def qd_copy(dest, came):
        start = pl.multiple_of(lax.rem(dest, shares) * own_tokens, own_tokens)
        return pltpu.make_async_remote_copy(
            src_ref=qd_pack.at[dest // shares, pl.ds(start, own_tokens)],
            dst_ref=qd_all.at[came],
            send_sem=qd_out.at[dest],
            recv_sem=qd_in.at[came],
            device_id={"ctx": dest},
            device_id_type=MESH,
        )

    def qo_copy(dest, came):
        return pltpu.make_async_remote_copy(
            src_ref=qo_put.at[dest],
            dst_ref=qo_got.at[came],
            send_sem=qo_out.at[dest],
            recv_sem=qo_in.at[came],
            device_id={"ctx": dest},
            device_id_type=MESH,
        )

    for make in (kv_copy, qd_copy):
        for step in range(1, count):
            make(lax.rem(me + count - step, count), me).start()
    for step in range(1, count):
        peer = lax.rem(me + step, count)
        kv_copy(peer, peer).wait_recv()

    lane = lax.broadcasted_iota(jnp.int32, (BLOCK, PAIR), 1)
    low = lane < HEAD_DIM
    row_lane = lax.broadcasted_iota(jnp.int32, (1, PAIR), 1)
    contract_last = (((1,), (1,)), ((), ()))
    contract_first = (((0,), (0,)), ((), ()))

    def front(peer, part):
        block = peer * blocks + my_share * own_blocks + part
        slot = peer * own_blocks + part
        qd = qd_all[peer, part * BLOCK : (part + 1) * BLOCK, :]
        near = [lax.rem(block + all_blocks - 1, all_blocks), lax.rem(block + 1, all_blocks), block]
        places = near + [
            ids_ref[slot * (GLOBALS + ROUNDS) + kind] for kind in range(GLOBALS + ROUNDS)
        ]
        kv = jnp.concatenate(
            [kv_all[p] for p in places], axis=0
        )
        zero = jnp.zeros_like(qd)
        diag = jnp.concatenate(
            [jnp.where(low, qd * jnp.bfloat16(SCALE), zero), jnp.where(low, zero, qd)], axis=0
        )
        both = lax.dot_general(diag, kv, contract_last, preferred_element_type=jnp.float32)
        scores = both[:BLOCK]
        dprob = both[BLOCK:]
        bias = jnp.where(
            row_lane < BLOCK,
            jnp.where(block == 0, NEG_FILL, 0.0),
            jnp.where(block == all_blocks - 1, NEG_FILL, 0.0),
        ).astype(jnp.float32)
        scores = lanes_joined(scores[:, :PAIR] + bias, scores[:, PAIR:])
        row_max = jnp.max(scores, axis=1, keepdims=True)
        weights = jnp.exp(scores - row_max)
        probs = weights * (1.0 / jnp.sum(weights, axis=1, keepdims=True))
        probs_b = probs.astype(jnp.bfloat16)
        attended = jnp.dot(probs_b, kv, preferred_element_type=jnp.float32).astype(jnp.bfloat16)
        row_dot = jnp.sum(
            jnp.where(low, 0.0, qd.astype(jnp.float32) * attended.astype(jnp.float32)),
            axis=1,
            keepdims=True,
        )
        dscore = (probs * (dprob - row_dot)).astype(jnp.bfloat16)
        grad_q = jnp.dot(dscore, kv, preferred_element_type=jnp.float32) * SCALE
        qo_put[peer, part * BLOCK : (part + 1) * BLOCK, :] = jnp.where(
            low, grad_q.astype(jnp.bfloat16), attended
        )
        terms = lax.dot_general(
            jnp.concatenate([dscore, probs_b], axis=0),
            diag,
            contract_first,
            preferred_element_type=jnp.float32,
        )
        width = ROUNDS * BLOCK
        rand_ref[pl.ds(pl.multiple_of(slot * width, width), width), :] = terms[
            (3 + GLOBALS) * BLOCK :
        ].astype(jnp.bfloat16)
        return near, terms

    def step_of(step, carry):
        peer = lax.rem(me + step, count)

        @pl.when(step > 0)
        def _():
            qd_copy(peer, peer).wait_recv()

        done = [front(peer, part) for part in range(own_blocks)]
        for near, terms in done:
            for kind in range(3):
                spot = pl.ds(pl.multiple_of(near[kind] * BLOCK, BLOCK), BLOCK)
                acc_ref[spot, :] += terms[kind * BLOCK : (kind + 1) * BLOCK]
        shared = [terms[3 * BLOCK : (3 + GLOBALS) * BLOCK] for _, terms in done]
        glob_ref[...] += functools.reduce(jnp.add, shared)

        @pl.when(step > 1)
        def _():
            qo_copy(lax.rem(me + step - 1, count), me).start()

        return carry

    lax.fori_loop(0, count, step_of, 0)
    qo_copy(lax.rem(me + count - 1, count), me).start()
    qo_got[me] = qo_put[me]
    for step in range(1, count):
        peer = lax.rem(me + step, count)
        kv_copy(peer, me).wait_send()
        qd_copy(peer, me).wait_send()
        qo_copy(peer, me).wait_send()
        qo_copy(peer, peer).wait_recv()


def sum_kernel(slots, shares, ids_ref, acc_in, glob_ref, rand_ref, qo_ref, gkv_ref, att_ref, gq_ref, acc_ref):
    acc_ref[...] = acc_in[...]
    for index in range(GLOBALS):
        spot = pl.ds(pl.multiple_of(ids_ref[index] * BLOCK, BLOCK), BLOCK)
        acc_ref[spot, :] += glob_ref[index * BLOCK : (index + 1) * BLOCK, :]

    def step(slot, carry):
        for kind in range(ROUNDS):
            place = ids_ref[slot * (GLOBALS + ROUNDS) + GLOBALS + kind]
            spot = pl.ds(pl.multiple_of(place * BLOCK, BLOCK), BLOCK)
            came = pl.ds(pl.multiple_of((slot * ROUNDS + kind) * BLOCK, BLOCK), BLOCK)
            acc_ref[spot, :] += rand_ref[came, :].astype(jnp.float32)
        return carry

    lax.fori_loop(0, slots, step, 0)
    gkv_ref[...] = acc_ref[...].astype(gkv_ref.dtype)
    own_tokens = qo_ref.shape[1]
    pairs = qo_ref.shape[0] // shares // 2
    for pair in range(pairs):
        cols = slice(pair * PAIR, (pair + 1) * PAIR)
        for share in range(shares):
            rows = slice(share * own_tokens, (share + 1) * own_tokens)
            even = qo_ref[2 * pair * shares + share]
            odd = qo_ref[(2 * pair + 1) * shares + share]
            gq_ref[rows, cols] = lanes_joined(even[:, :HEAD_DIM], odd[:, :HEAD_DIM])
            att_ref[rows, cols] = lanes_joined(even[:, HEAD_DIM:], odd[:, HEAD_DIM:])


def return_kernel(count, shares, gkv_ref, gk_ref, gv_ref, got, out_sem, in_sem):
    me = lax.axis_index("ctx")
    tokens = got.shape[1]
    barrier = greet(me, count)
    pl.semaphore_wait(barrier, count - 1)

    def copy(dest, came):
        return pltpu.make_async_remote_copy(
            src_ref=gkv_ref.at[dest],
            dst_ref=got.at[came],
            send_sem=out_sem.at[dest],
            recv_sem=in_sem.at[came],
            device_id={"ctx": dest},
            device_id_type=MESH,
        )

    for step in range(1, count):
        copy(lax.rem(me + count - step, count), me).start()
    got[me] = gkv_ref[me]
    for step in range(1, count):
        peer = lax.rem(me + step, count)
        copy(peer, me).wait_send()
        copy(peer, peer).wait_recv()

    def head_of(head):
        total = got[head * shares]
        if shares > 1:
            total = total.astype(jnp.float32)
            for share in range(1, shares):
                total += got[head * shares + share].astype(jnp.float32)
            total = total.astype(jnp.bfloat16)
        return total

    for pair in range(count // shares // 2):
        cols = slice(pair * PAIR, (pair + 1) * PAIR)
        even = head_of(2 * pair)
        odd = head_of(2 * pair + 1)
        gk_ref[:, cols] = lanes_joined(even[:, :HEAD_DIM], odd[:, :HEAD_DIM])
        gv_ref[:, cols] = lanes_joined(even[:, HEAD_DIM:], odd[:, HEAD_DIM:])


VMEM = pl.BlockSpec(memory_space=pltpu.VMEM)
SMEM = pl.BlockSpec(memory_space=pltpu.SMEM)


def per_device(query, key, value, cotangent, global_ids, rand_owner, rand_local):
    tokens, features = query.shape
    blocks = tokens // BLOCK
    heads = features // HEAD_DIM
    groups = heads // GROUP_HEADS
    count = lax.axis_size("ctx")
    me = lax.axis_index("ctx")
    shares = count // heads
    own_blocks = blocks // shares
    own_tokens = own_blocks * BLOCK
    all_blocks = count * blocks
    slots = count * own_blocks
    shape = jax.ShapeDtypeStruct
    bf16, f32 = jnp.bfloat16, jnp.float32

    my_group = me // shares // GROUP_HEADS
    picked = (rand_owner * blocks + rand_local).reshape(
        count, shares, own_blocks, groups, ROUNDS
    )
    picked = lax.dynamic_index_in_dim(picked, my_group, 3, keepdims=False)
    picked = lax.dynamic_index_in_dim(picked, me % shares, 1, keepdims=False)
    picked = picked.reshape(slots, ROUNDS)
    shared = jnp.broadcast_to(global_ids[None, :], (slots, GLOBALS))
    ids = jnp.concatenate([shared, picked], axis=1).astype(jnp.int32).reshape(-1)

    dma = pltpu.SemaphoreType.DMA((count,))
    qo, acc, glob, rand = pl.pallas_call(
        functools.partial(attend_kernel, count, shares),
        out_shape=(
            shape((count, own_tokens, PAIR), bf16),
            shape((count * tokens, PAIR), f32),
            shape((GLOBALS * BLOCK, PAIR), f32),
            shape((slots * ROUNDS * BLOCK, PAIR), bf16),
        ),
        in_specs=[SMEM] + [VMEM] * 4,
        out_specs=(VMEM,) * 4,
        scratch_shapes=[
            pltpu.VMEM((heads, tokens, PAIR), bf16),
            pltpu.VMEM((heads, tokens, PAIR), bf16),
            pltpu.VMEM((all_blocks, BLOCK, PAIR), bf16),
            pltpu.VMEM((count, own_tokens, PAIR), bf16),
            pltpu.VMEM((count, own_tokens, PAIR), bf16),
        ]
        + [dma] * 6,
        compiler_params=pltpu.CompilerParams(
            collective_id=0, has_side_effects=True, vmem_limit_bytes=40 * 1024 * 1024
        ),
        name="attend",
    )(ids, query, key, value, cotangent)
    flat = shape((tokens, features), bf16)
    gkv, attended, grad_query = pl.pallas_call(
        functools.partial(sum_kernel, slots, shares),
        out_shape=(shape((count * tokens, PAIR), bf16), flat, flat),
        in_specs=[SMEM] + [VMEM] * 4,
        out_specs=(VMEM,) * 3,
        scratch_shapes=[pltpu.VMEM((count * tokens, PAIR), f32)],
        compiler_params=pltpu.CompilerParams(vmem_limit_bytes=32 * 1024 * 1024),
        name="total",
    )(ids, acc, glob, rand, qo)
    grad_key, grad_value = pl.pallas_call(
        functools.partial(return_kernel, count, shares),
        out_shape=(flat, flat),
        in_specs=[VMEM],
        out_specs=(VMEM,) * 2,
        scratch_shapes=[pltpu.VMEM((count, tokens, PAIR), bf16), dma, dma],
        compiler_params=pltpu.CompilerParams(
            collective_id=1, has_side_effects=True, vmem_limit_bytes=16 * 1024 * 1024
        ),
        name="back",
    )(gkv.reshape(count, tokens, PAIR))
    return attended, grad_query, grad_key, grad_value


def solution(mesh):
    rows = P(("groups", "ctx"), None)
    return jax.shard_map(
        per_device,
        mesh=mesh,
        in_specs=(rows, rows, rows, rows, P("groups"), P("groups", None), P("groups", None)),
        out_specs=(rows,) * 4,
        check_vma=False,
    )
```

time: 177 us -> 136 us (0.77)
  blocking collectives: 93.1 us -> 0 us
  Pallas kernels: 54.4 us -> 127 us
  waiting for transfers between devices: 20.9 us -> 0 us
  starting transfers between devices: 5.03 us -> 0 us
  local copies, waits for them, and re-layouts: 1.85 us -> 6.83 us
    all_to_all x3 -> x0, blocking collectives: 93.1 us -> none  [the longest x1 32.1 us: per_device(): qd_all = exchange(qd_send).reshape(count * own_tokens, PAIR)]
    pallas_call x3, Pallas kernels: 54.4 us -> 127 us  [the longest x1 94.3 us: per_device(): pl.pallas_call(functools.partial(attend_kernel, count, shares), out_shape...]
    all_to_all x1 -> x0, waiting for transfers between devices: 20.9 us -> none  [per_device(): kv_all = exchange(kv_send).reshape(count * tokens, PAIR)]
    all_to_all x1 -> x0, starting transfers between devices: 5.03 us -> none  [per_device(): kv_all = exchange(kv_send).reshape(count * tokens, PAIR)]
    unnamed x6 -> x10, local copies, waits for them, and re-layouts: 1.32 us -> 5.75 us
  transfers between devices with their start and end apart: 1 -> 0, of which waited for: 1 -> 0; matrix products, arithmetic and copies ran while one was open for 0% -> 0% of each run, Pallas kernels for 0% -> 0%
where the time goes in v2:
time: 136 us
  Pallas kernels  127 us (93%)
  local copies, waits for them, and re-layouts  6.83 us (5%)
    pallas_call x1, Pallas kernels, per_device(): pl.pallas_call(functools.partial(attend_kernel, count, shares), out_shape...  94.3 us
    pallas_call x1, Pallas kernels, per_device(): pl.pallas_call(functools.partial(return_kernel, count, shares), out_shape...  29.4 us
    unnamed x10, local copies, waits for them, and re-layouts  5.75 us
    pallas_call x1, Pallas kernels, per_device(): pl.pallas_call(functools.partial(sum_kernel, slots, shares), out_shape=(s...  3.54 us

profile of v2, /device:TPU:0, one launch (start us, length us, event | category | flops | bytes accessed | tf_op | source)
XLA Modules:
  0.0 135.5 jit_solution(17814979640305740144)
XLA Ops:
  0.6 0.7 pad.clone
  1.3 0.7 multiply_add_fusion
  2.0 0.1 reshape.23
  2.1 0.1 reshape.24
  2.2 0.1 pad_add_fusion
  2.3 0.1 copy.11
  2.4 0.1 reshape.25.ids_ref
  2.5 0.0 copy-start
  2.5 1.0 copy-done
  3.6 0.0 copy-start.1
  3.6 1.0 copy-done.1
  4.6 0.0 copy-start.2
  4.6 1.0 copy-done.2
  5.7 0.0 copy-start.3
  5.7 1.0 copy-done.3
  6.7 94.3 %attend.1 = (bf16[16,256,128]{2,1,0:T(8,128)(2,1)S(1)}, f32[4096,128]{1,0:T(8,128)S(1)}, f32[128,128]{1,0:T(8,128)S(1)}, bf16[12288,128]{1,0:T(8,128)(2,1)S(1)}) custom-call(s32[320]{0:T(512)S(1)} %reshape.25.ids_ref, bf16[256,1024]{1,0:T(8,128)(2,1)S(1)} %copy-done, bf16[256,1024]{1,0:T(8,128)(2,1)S(1)} %copy-done.1, bf16[256,1024]{1,0:T(8,128)(2,1)S(1)} %copy-done.2, ...), custom_call_target="tpu_custom_call" | custom-call | tf_op jit(solution)/shard_map/attend/pallas_call | solution.py:309
  101.0 3.5 %total.1 = (bf16[4096,128]{1,0:T(8,128)(2,1)S(1)}, bf16[256,1024]{1,0:T(8,128)(2,1)}, bf16[256,1024]{1,0:T(8,128)(2,1)}) custom-call(s32[320]{0:T(512)S(1)} %reshape.25.ids_ref, f32[4096,128]{1,0:T(8,128)S(1)} %get-tuple-element.13.acc_in, f32[128,128]{1,0:T(8,128)S(1)} %get-tuple-element.14.glob_ref, bf16[12288,128]{1,0:T(8,128)(2,1)S(1)} %get-tuple-element.15.rand_ref, ...), custom_call_target="tpu_custom_call" | custom-call | tf_op jit(solution)/shard_map/total/pallas_call | solution.py:333
  104.5 29.4 %back.1 = (bf16[256,1024]{1,0:T(8,128)(2,1)S(1)}, bf16[256,1024]{1,0:T(8,128)(2,1)S(1)}) custom-call(bf16[16,256,128]{2,1,0:T(8,128)(2,1)S(1)} %bitcast.7), custom_call_target="tpu_custom_call" | custom-call | tf_op jit(solution)/shard_map/back/pallas_call | solution.py:342
  133.9 0.8 copy.14
  134.7 0.8 copy.15
  (1 shorter events, 0.0 us)
Async XLA Ops:
  2.5 1.0 copy-start
  3.6 1.0 copy-start.1
  4.6 1.0 copy-start.2
  5.7 1.0 copy-start.3

commit v3 on v2

--- a/solution.py
+++ b/solution.py
@@ -34,11 +34,13 @@
 def attend_kernel(
     count,
     shares,
-    ids_ref,
-    q_ref,
-    k_ref,
-    v_ref,
-    d_ref,
+    glob_ids,
+    owner_ref,
+    local_ref,
+    q_hbm,
+    k_hbm,
+    v_hbm,
+    d_hbm,
     qo_got,
     acc_ref,
     glob_ref,
@@ -48,6 +50,11 @@
     kv_all,
     qd_all,
     qo_put,
+    q_ref,
+    k_ref,
+    v_ref,
+    d_ref,
+    fetch,
     kv_out,
     kv_in,
     qd_out,
@@ -63,19 +70,30 @@
     all_blocks = count * blocks
     my_share = lax.rem(me, shares)
 
+    pulls = [
+        pltpu.make_async_copy(source, target, fetch.at[index])
+        for index, (source, target) in enumerate(
+            ((k_hbm, k_ref), (v_hbm, v_ref), (q_hbm, q_ref), (d_hbm, d_ref))
+        )
+    ]
+    for pull in pulls:
+        pull.start()
     barrier = greet(me, count)
-    for pair in range(heads // 2):
-        cols = slice(pair * PAIR, (pair + 1) * PAIR)
-        for left_ref, right_ref, out_ref in ((k_ref, v_ref, kv_pack), (q_ref, d_ref, qd_pack)):
+    my_head = me // shares
+    my_group = my_head // GROUP_HEADS
+    my_rows = pl.ds(pl.multiple_of(my_share * own_tokens, own_tokens), own_tokens)
+
+    def pack(left_ref, right_ref, out_ref):
+        for pair in range(heads // 2):
+            cols = slice(pair * PAIR, (pair + 1) * PAIR)
             left = left_ref[:, cols]
             right = right_ref[:, cols]
             out_ref[2 * pair] = lanes_joined(left[:, :HEAD_DIM], right[:, :HEAD_DIM])
             out_ref[2 * pair + 1] = lanes_joined(left[:, HEAD_DIM:], right[:, HEAD_DIM:])
-    my_head = me // shares
-    my_rows = pl.ds(pl.multiple_of(my_share * own_tokens, own_tokens), own_tokens)
-    for part in range(blocks):
-        kv_all[me * blocks + part] = kv_pack[my_head, part * BLOCK : (part + 1) * BLOCK]
-    qd_all[me] = qd_pack[my_head, my_rows, :]
+
+    pulls[0].wait()
+    pulls[1].wait()
+    pack(k_ref, v_ref, kv_pack)
     acc_ref[...] = jnp.zeros_like(acc_ref)
     glob_ref[...] = jnp.zeros_like(glob_ref)
     pl.semaphore_wait(barrier, count - 1)
@@ -111,12 +129,19 @@
             device_id_type=MESH,
         )
 
-    for make in (kv_copy, qd_copy):
-        for step in range(1, count):
-            make(lax.rem(me + count - step, count), me).start()
+    for step in range(1, count):
+        kv_copy(lax.rem(me + count - step, count), me).start()
+    for part in range(blocks):
+        kv_all[me * blocks + part] = kv_pack[my_head, part * BLOCK : (part + 1) * BLOCK]
+    pulls[2].wait()
+    pulls[3].wait()
+    pack(q_ref, d_ref, qd_pack)
+    qd_all[me] = qd_pack[my_head, my_rows, :]
     for step in range(1, count):
         peer = lax.rem(me + step, count)
         kv_copy(peer, peer).wait_recv()
+    for step in range(1, count):
+        qd_copy(lax.rem(me + count - step, count), me).start()
 
     lane = lax.broadcasted_iota(jnp.int32, (BLOCK, PAIR), 1)
     low = lane < HEAD_DIM
@@ -130,7 +155,11 @@
         qd = qd_all[peer, part * BLOCK : (part + 1) * BLOCK, :]
         near = [lax.rem(block + all_blocks - 1, all_blocks), lax.rem(block + 1, all_blocks), block]
         places = near + [
-            ids_ref[slot * (GLOBALS + ROUNDS) + kind] for kind in range(GLOBALS + ROUNDS)
+            glob_ids[kind] for kind in range(GLOBALS)
+        ] + [
+            owner_ref[block, my_group * ROUNDS + kind] * blocks
+            + local_ref[block, my_group * ROUNDS + kind]
+            for kind in range(ROUNDS)
         ]
         kv = jnp.concatenate(
             [kv_all[p] for p in places], axis=0
@@ -207,21 +236,43 @@
         qo_copy(peer, peer).wait_recv()
 
 
-def sum_kernel(slots, shares, ids_ref, acc_in, glob_ref, rand_ref, qo_ref, gkv_ref, att_ref, gq_ref, acc_ref):
+def sum_kernel(
+    count,
+    shares,
+    blocks,
+    glob_ids,
+    owner_ref,
+    local_ref,
+    acc_in,
+    glob_ref,
+    rand_ref,
+    qo_ref,
+    gkv_ref,
+    att_ref,
+    gq_ref,
+    acc_ref,
+):
+    me = lax.axis_index("ctx")
+    own_blocks = blocks // shares
+    first = lax.rem(me, shares) * own_blocks
+    column = me // shares // GROUP_HEADS * ROUNDS
     acc_ref[...] = acc_in[...]
     for index in range(GLOBALS):
-        spot = pl.ds(pl.multiple_of(ids_ref[index] * BLOCK, BLOCK), BLOCK)
+        spot = pl.ds(pl.multiple_of(glob_ids[index] * BLOCK, BLOCK), BLOCK)
         acc_ref[spot, :] += glob_ref[index * BLOCK : (index + 1) * BLOCK, :]
 
-    def step(slot, carry):
-        for kind in range(ROUNDS):
-            place = ids_ref[slot * (GLOBALS + ROUNDS) + GLOBALS + kind]
-            spot = pl.ds(pl.multiple_of(place * BLOCK, BLOCK), BLOCK)
-            came = pl.ds(pl.multiple_of((slot * ROUNDS + kind) * BLOCK, BLOCK), BLOCK)
-            acc_ref[spot, :] += rand_ref[came, :].astype(jnp.float32)
+    def step(peer, carry):
+        for part in range(own_blocks):
+            block = peer * blocks + first + part
+            slot = peer * own_blocks + part
+            for kind in range(ROUNDS):
+                place = owner_ref[block, column + kind] * blocks + local_ref[block, column + kind]
+                spot = pl.ds(pl.multiple_of(place * BLOCK, BLOCK), BLOCK)
+                came = pl.ds(pl.multiple_of((slot * ROUNDS + kind) * BLOCK, BLOCK), BLOCK)
+                acc_ref[spot, :] += rand_ref[came, :].astype(jnp.float32)
         return carry
 
-    lax.fori_loop(0, slots, step, 0)
+    lax.fori_loop(0, count, step, 0)
     gkv_ref[...] = acc_ref[...].astype(gkv_ref.dtype)
     own_tokens = qo_ref.shape[1]
     pairs = qo_ref.shape[0] // shares // 2
@@ -254,12 +305,15 @@
     for step in range(1, count):
         copy(lax.rem(me + count - step, count), me).start()
     got[me] = gkv_ref[me]
-    for step in range(1, count):
-        peer = lax.rem(me + step, count)
-        copy(peer, me).wait_send()
-        copy(peer, peer).wait_recv()
 
     def head_of(head):
+        for share in range(shares):
+            source = head * shares + share
+
+            @pl.when(source != me)
+            def _():
+                copy(source, source).wait_recv()
+
         total = got[head * shares]
         if shares > 1:
             total = total.astype(jnp.float32)
@@ -274,6 +328,8 @@
         odd = head_of(2 * pair + 1)
         gk_ref[:, cols] = lanes_joined(even[:, :HEAD_DIM], odd[:, :HEAD_DIM])
         gv_ref[:, cols] = lanes_joined(even[:, HEAD_DIM:], odd[:, HEAD_DIM:])
+    for step in range(1, count):
+        copy(lax.rem(me + step, count), me).wait_send()
 
 
 VMEM = pl.BlockSpec(memory_space=pltpu.VMEM)
@@ -284,9 +340,7 @@
     tokens, features = query.shape
     blocks = tokens // BLOCK
     heads = features // HEAD_DIM
-    groups = heads // GROUP_HEADS
     count = lax.axis_size("ctx")
-    me = lax.axis_index("ctx")
     shares = count // heads
     own_blocks = blocks // shares
     own_tokens = own_blocks * BLOCK
@@ -294,16 +348,6 @@
     slots = count * own_blocks
     shape = jax.ShapeDtypeStruct
     bf16, f32 = jnp.bfloat16, jnp.float32
-
-    my_group = me // shares // GROUP_HEADS
-    picked = (rand_owner * blocks + rand_local).reshape(
-        count, shares, own_blocks, groups, ROUNDS
-    )
-    picked = lax.dynamic_index_in_dim(picked, my_group, 3, keepdims=False)
-    picked = lax.dynamic_index_in_dim(picked, me % shares, 1, keepdims=False)
-    picked = picked.reshape(slots, ROUNDS)
-    shared = jnp.broadcast_to(global_ids[None, :], (slots, GLOBALS))
-    ids = jnp.concatenate([shared, picked], axis=1).astype(jnp.int32).reshape(-1)
 
     dma = pltpu.SemaphoreType.DMA((count,))
     qo, acc, glob, rand = pl.pallas_call(
@@ -314,7 +358,7 @@
             shape((GLOBALS * BLOCK, PAIR), f32),
             shape((slots * ROUNDS * BLOCK, PAIR), bf16),
         ),
-        in_specs=[SMEM] + [VMEM] * 4,
+        in_specs=[SMEM] * 3 + [pl.BlockSpec(memory_space=pl.ANY)] * 4,
         out_specs=(VMEM,) * 4,
         scratch_shapes=[
             pltpu.VMEM((heads, tokens, PAIR), bf16),
@@ -323,22 +367,24 @@
             pltpu.VMEM((count, own_tokens, PAIR), bf16),
             pltpu.VMEM((count, own_tokens, PAIR), bf16),
         ]
+        + [pltpu.VMEM((tokens, features), bf16)] * 4
+        + [pltpu.SemaphoreType.DMA((4,))]
         + [dma] * 6,
         compiler_params=pltpu.CompilerParams(
             collective_id=0, has_side_effects=True, vmem_limit_bytes=40 * 1024 * 1024
         ),
         name="attend",
-    )(ids, query, key, value, cotangent)
+    )(global_ids, rand_owner, rand_local, query, key, value, cotangent)
     flat = shape((tokens, features), bf16)
     gkv, attended, grad_query = pl.pallas_call(
-        functools.partial(sum_kernel, slots, shares),
+        functools.partial(sum_kernel, count, shares, blocks),
         out_shape=(shape((count * tokens, PAIR), bf16), flat, flat),
-        in_specs=[SMEM] + [VMEM] * 4,
+        in_specs=[SMEM] * 3 + [VMEM] * 4,
         out_specs=(VMEM,) * 3,
         scratch_shapes=[pltpu.VMEM((count * tokens, PAIR), f32)],
         compiler_params=pltpu.CompilerParams(vmem_limit_bytes=32 * 1024 * 1024),
         name="total",
-    )(ids, acc, glob, rand, qo)
+    )(global_ids, rand_owner, rand_local, acc, glob, rand, qo)
     grad_key, grad_value = pl.pallas_call(
         functools.partial(return_kernel, count, shares),
         out_shape=(flat, flat),

time: 136 us -> 133 us (0.978)
  Pallas kernels: 127 us -> 124 us
    pallas_call x1, Pallas kernels: 94.3 us -> 90.4 us  [per_device(): pl.pallas_call(functools.partial(attend_kernel, count, shares), out_shape...]
    unnamed x10 -> x14, local copies, waits for them, and re-layouts: 5.75 us -> 7.96 us
where the time goes in v3:
time: 133 us
  Pallas kernels  124 us (93%)
  local copies, waits for them, and re-layouts  7.96 us (6%)
    pallas_call x1, Pallas kernels, per_device(): pl.pallas_call(functools.partial(attend_kernel, count, shares), out_shape...  90.4 us
    pallas_call x1, Pallas kernels, per_device(): pl.pallas_call(functools.partial(return_kernel, count, shares), out_shape...  29.6 us
    unnamed x14, local copies, waits for them, and re-layouts  7.96 us
    pallas_call x1, Pallas kernels, per_device(): pl.pallas_call(functools.partial(sum_kernel, count, shares, blocks), out_...  4.48 us

profile of v3, /device:TPU:0, one launch (start us, length us, event | category | flops | bytes accessed | tf_op | source)
XLA Modules:
  0.0 133.1 jit_solution(1161593843200463246)
XLA Ops:
  0.6 0.8 copy.13.owner_ref
  1.4 0.8 copy.14.local_ref
  2.2 0.0 copy-start
  2.2 1.0 copy-done
  3.2 0.0 copy-start.1
  3.2 1.0 copy-done.1
  4.3 0.0 copy-start.2
  4.3 1.0 copy-done.2
  5.3 0.0 copy-start.3
  5.3 1.0 copy-done.3
  6.4 0.0 copy-start.4
  6.4 0.7 copy-done.4
  7.0 90.4 %attend.1 = (bf16[16,256,128]{2,1,0:T(8,128)(2,1)S(1)}, f32[4096,128]{1,0:T(8,128)S(1)}, f32[128,128]{1,0:T(8,128)S(1)}, bf16[12288,128]{1,0:T(8,128)(2,1)S(1)}) custom-call(s32[2]{0:T(128)S(1)} %copy-done.4, s32[64,6]{1,0:T(8,128)S(1)} %copy.13.owner_ref, s32[64,6]{1,0:T(8,128)S(1)} %copy.14.local_ref, bf16[256,1024]{1,0:T(8,128)(2,1)S(1)} %copy-done, ...), custom_call_target="tpu_custom_call" | custom-call | tf_op jit(solution)/shard_map/attend/pallas_call | solution.py:353
  97.4 4.5 %total.1 = (bf16[4096,128]{1,0:T(8,128)(2,1)S(1)}, bf16[256,1024]{1,0:T(8,128)(2,1)}, bf16[256,1024]{1,0:T(8,128)(2,1)}) custom-call(s32[2]{0:T(128)S(1)} %copy-done.4, s32[64,6]{1,0:T(8,128)S(1)} %copy.13.owner_ref, s32[64,6]{1,0:T(8,128)S(1)} %copy.14.local_ref, f32[4096,128]{1,0:T(8,128)S(1)} %get-tuple-element.13.acc_in, ...), custom_call_target="tpu_custom_call" | custom-call | tf_op jit(solution)/shard_map/total/pallas_call | solution.py:379
  101.9 29.6 %back.1 = (bf16[256,1024]{1,0:T(8,128)(2,1)S(1)}, bf16[256,1024]{1,0:T(8,128)(2,1)S(1)}) custom-call(bf16[16,256,128]{2,1,0:T(8,128)(2,1)S(1)} %bitcast.1), custom_call_target="tpu_custom_call" | custom-call | tf_op jit(solution)/shard_map/back/pallas_call | solution.py:388
  131.5 0.8 copy.17
  132.3 0.8 copy.18
Async XLA Ops:
  2.2 1.0 copy-start
  3.2 1.0 copy-start.1
  4.3 1.0 copy-start.2
  5.3 1.0 copy-start.3
  6.4 0.7 copy-start.4

commit v4 on v3

--- a/solution.py
+++ b/solution.py
@@ -157,8 +157,8 @@
         places = near + [
             glob_ids[kind] for kind in range(GLOBALS)
         ] + [
-            owner_ref[block, my_group * ROUNDS + kind] * blocks
-            + local_ref[block, my_group * ROUNDS + kind]
+            owner_ref[my_group * ROUNDS + kind, block] * blocks
+            + local_ref[my_group * ROUNDS + kind, block]
             for kind in range(ROUNDS)
         ]
         kv = jnp.concatenate(
@@ -266,7 +266,7 @@
             block = peer * blocks + first + part
             slot = peer * own_blocks + part
             for kind in range(ROUNDS):
-                place = owner_ref[block, column + kind] * blocks + local_ref[block, column + kind]
+                place = owner_ref[column + kind, block] * blocks + local_ref[column + kind, block]
                 spot = pl.ds(pl.multiple_of(place * BLOCK, BLOCK), BLOCK)
                 came = pl.ds(pl.multiple_of((slot * ROUNDS + kind) * BLOCK, BLOCK), BLOCK)
                 acc_ref[spot, :] += rand_ref[came, :].astype(jnp.float32)
@@ -358,7 +358,7 @@
             shape((GLOBALS * BLOCK, PAIR), f32),
             shape((slots * ROUNDS * BLOCK, PAIR), bf16),
         ),
-        in_specs=[SMEM] * 3 + [pl.BlockSpec(memory_space=pl.ANY)] * 4,
+        in_specs=[SMEM] * 3 + [pl.BlockSpec(memory_space=pltpu.HBM)] * 4,
         out_specs=(VMEM,) * 4,
         scratch_shapes=[
             pltpu.VMEM((heads, tokens, PAIR), bf16),
@@ -374,7 +374,7 @@
             collective_id=0, has_side_effects=True, vmem_limit_bytes=40 * 1024 * 1024
         ),
         name="attend",
-    )(global_ids, rand_owner, rand_local, query, key, value, cotangent)
+    )(global_ids, rand_owner.T, rand_local.T, query, key, value, cotangent)
     flat = shape((tokens, features), bf16)
     gkv, attended, grad_query = pl.pallas_call(
         functools.partial(sum_kernel, count, shares, blocks),
@@ -384,7 +384,7 @@
         scratch_shapes=[pltpu.VMEM((count * tokens, PAIR), f32)],
         compiler_params=pltpu.CompilerParams(vmem_limit_bytes=32 * 1024 * 1024),
         name="total",
-    )(global_ids, rand_owner, rand_local, acc, glob, rand, qo)
+    )(global_ids, rand_owner.T, rand_local.T, acc, glob, rand, qo)
     grad_key, grad_value = pl.pallas_call(
         functools.partial(return_kernel, count, shares),
         out_shape=(flat, flat),

time: 133 us -> 131 us (0.985)
    unnamed x14 -> x16, local copies, waits for them, and re-layouts: 7.96 us -> 7.77 us
where the time goes in v4:
time: 131 us
  Pallas kernels  123 us (94%)
  local copies, waits for them, and re-layouts  7.77 us (6%)
    pallas_call x1, Pallas kernels, per_device(): pl.pallas_call(functools.partial(attend_kernel, count, shares), out_shape...  89.5 us
    pallas_call x1, Pallas kernels, per_device(): pl.pallas_call(functools.partial(return_kernel, count, shares), out_shape...  29.6 us
    unnamed x16, local copies, waits for them, and re-layouts  7.77 us
    pallas_call x1, Pallas kernels, per_device(): pl.pallas_call(functools.partial(sum_kernel, count, shares, blocks), out_...  3.49 us

profile of v4, /device:TPU:0, one launch (start us, length us, event | category | flops | bytes accessed | tf_op | source)
XLA Modules:
  0.0 131.0 jit_solution(3911289676741669659)
XLA Ops:
  0.6 0.0 copy-start
  0.6 1.0 copy-done
  1.7 0.0 copy-start.1
  1.7 1.0 copy-done.1
  2.7 0.0 copy-start.2
  2.7 1.0 copy-done.2
  3.8 0.0 copy-start.3
  3.8 1.0 copy-done.3
  4.8 0.0 copy-start.4
  4.8 0.7 copy-done.4
  5.5 0.0 copy-start.5
  5.5 0.7 copy-done.5
  6.2 0.0 copy-start.6
  6.2 0.7 copy-done.6
  6.8 89.5 %attend.1 = (bf16[16,256,128]{2,1,0:T(8,128)(2,1)S(1)}, f32[4096,128]{1,0:T(8,128)S(1)}, f32[128,128]{1,0:T(8,128)S(1)}, bf16[12288,128]{1,0:T(8,128)(2,1)S(1)}) custom-call(s32[2]{0:T(128)S(1)} %copy-done.6, s32[6,64]{1,0:T(8,128)S(1)} %bitcast.4, s32[6,64]{1,0:T(8,128)S(1)} %bitcast.6, bf16[256,1024]{1,0:T(8,128)(2,1)S(1)} %copy-done, ...), custom_call_target="tpu_custom_call" | custom-call | tf_op jit(solution)/shard_map/attend/pallas_call | solution.py:353
  96.3 3.5 %total.1 = (bf16[4096,128]{1,0:T(8,128)(2,1)S(1)}, bf16[256,1024]{1,0:T(8,128)(2,1)}, bf16[256,1024]{1,0:T(8,128)(2,1)}) custom-call(s32[2]{0:T(128)S(1)} %copy-done.6, s32[6,64]{1,0:T(8,128)S(1)} %bitcast.5, s32[6,64]{1,0:T(8,128)S(1)} %bitcast.7, f32[4096,128]{1,0:T(8,128)S(1)} %get-tuple-element.13.acc_in, f32[128,128]{1,0:T(8,128)S(1)} %get-tuple-element.14.glob_ref, ...), custom_call_target="tpu_custom_call" | custom-call | tf_op jit(solution)/shard_map/total/pallas_call | solution.py:379
  99.8 29.6 %back.1 = (bf16[256,1024]{1,0:T(8,128)(2,1)S(1)}, bf16[256,1024]{1,0:T(8,128)(2,1)S(1)}) custom-call(bf16[16,256,128]{2,1,0:T(8,128)(2,1)S(1)} %bitcast.3), custom_call_target="tpu_custom_call" | custom-call | tf_op jit(solution)/shard_map/back/pallas_call | solution.py:388
  129.4 0.8 copy.13
  130.2 0.8 copy.14
Async XLA Ops:
  0.6 1.0 copy-start
  1.7 1.0 copy-start.1
  2.7 1.0 copy-start.2
  3.8 1.0 copy-start.3
  4.8 0.7 copy-start.4
  5.5 0.7 copy-start.5
  6.2 0.7 copy-start.6

commit v5 on v4

--- a/solution.py
+++ b/solution.py
@@ -149,9 +149,8 @@
     contract_last = (((1,), (1,)), ((), ()))
     contract_first = (((0,), (0,)), ((), ()))
 
-    def front(peer, part):
+    def load(peer, part):
         block = peer * blocks + my_share * own_blocks + part
-        slot = peer * own_blocks + part
         qd = qd_all[peer, part * BLOCK : (part + 1) * BLOCK, :]
         near = [lax.rem(block + all_blocks - 1, all_blocks), lax.rem(block + 1, all_blocks), block]
         places = near + [
@@ -161,16 +160,16 @@
             + local_ref[my_group * ROUNDS + kind, block]
             for kind in range(ROUNDS)
         ]
-        kv = jnp.concatenate(
-            [kv_all[p] for p in places], axis=0
-        )
+        kv = jnp.concatenate([kv_all[p] for p in places], axis=0)
         zero = jnp.zeros_like(qd)
         diag = jnp.concatenate(
             [jnp.where(low, qd * jnp.bfloat16(SCALE), zero), jnp.where(low, zero, qd)], axis=0
         )
         both = lax.dot_general(diag, kv, contract_last, preferred_element_type=jnp.float32)
+        return block, near, qd, kv, diag, both
+
+    def soften(block, both):
         scores = both[:BLOCK]
-        dprob = both[BLOCK:]
         bias = jnp.where(
             row_lane < BLOCK,
             jnp.where(block == 0, NEG_FILL, 0.0),
@@ -180,14 +179,16 @@
         row_max = jnp.max(scores, axis=1, keepdims=True)
         weights = jnp.exp(scores - row_max)
         probs = weights * (1.0 / jnp.sum(weights, axis=1, keepdims=True))
-        probs_b = probs.astype(jnp.bfloat16)
-        attended = jnp.dot(probs_b, kv, preferred_element_type=jnp.float32).astype(jnp.bfloat16)
+        return probs, probs.astype(jnp.bfloat16)
+
+    def finish(peer, part, qd, kv, diag, both, probs, probs_b, attended):
+        slot = peer * own_blocks + part
         row_dot = jnp.sum(
             jnp.where(low, 0.0, qd.astype(jnp.float32) * attended.astype(jnp.float32)),
             axis=1,
             keepdims=True,
         )
-        dscore = (probs * (dprob - row_dot)).astype(jnp.bfloat16)
+        dscore = (probs * (both[BLOCK:] - row_dot)).astype(jnp.bfloat16)
         grad_q = jnp.dot(dscore, kv, preferred_element_type=jnp.float32) * SCALE
         qo_put[peer, part * BLOCK : (part + 1) * BLOCK, :] = jnp.where(
             low, grad_q.astype(jnp.bfloat16), attended
@@ -202,7 +203,19 @@
         rand_ref[pl.ds(pl.multiple_of(slot * width, width), width), :] = terms[
             (3 + GLOBALS) * BLOCK :
         ].astype(jnp.bfloat16)
-        return near, terms
+        return terms
+
+    def front(peer):
+        stage = [load(peer, part) for part in range(own_blocks)]
+        soft = [soften(block, both) for block, _, _, _, _, both in stage]
+        seen = [
+            jnp.dot(probs_b, kept[3], preferred_element_type=jnp.float32).astype(jnp.bfloat16)
+            for kept, (_, probs_b) in zip(stage, soft)
+        ]
+        return [
+            (near, finish(peer, part, qd, kv, diag, both, *soft[part], seen[part]))
+            for part, (block, near, qd, kv, diag, both) in enumerate(stage)
+        ]
 
     def step_of(step, carry):
         peer = lax.rem(me + step, count)
@@ -211,7 +224,7 @@
         def _():
             qd_copy(peer, peer).wait_recv()
 
-        done = [front(peer, part) for part in range(own_blocks)]
+        done = front(peer)
         for near, terms in done:
             for kind in range(3):
                 spot = pl.ds(pl.multiple_of(near[kind] * BLOCK, BLOCK), BLOCK)

time: 131 us -> 128 us (0.977)
  Pallas kernels: 123 us -> 120 us
    pallas_call x1, Pallas kernels: 89.5 us -> 82 us  [per_device(): pl.pallas_call(functools.partial(attend_kernel, count, shares), out_shape...]
    pallas_call x1, Pallas kernels: 29.6 us -> 34 us  [per_device(): pl.pallas_call(functools.partial(return_kernel, count, shares), out_shape...]
where the time goes in v5:
time: 128 us
  Pallas kernels  120 us (94%)
  local copies, waits for them, and re-layouts  7.77 us (6%)
    pallas_call x1, Pallas kernels, per_device(): pl.pallas_call(functools.partial(attend_kernel, count, shares), out_shape...  82 us
    pallas_call x1, Pallas kernels, per_device(): pl.pallas_call(functools.partial(return_kernel, count, shares), out_shape...  34 us
    unnamed x16, local copies, waits for them, and re-layouts  7.77 us
    pallas_call x1, Pallas kernels, per_device(): pl.pallas_call(functools.partial(sum_kernel, count, shares, blocks), out_...  3.49 us

profile of v5, /device:TPU:0, one launch (start us, length us, event | category | flops | bytes accessed | tf_op | source)
XLA Modules:
  0.0 128.0 jit_solution(15194038266618007503)
XLA Ops:
  0.6 0.0 copy-start
  0.6 1.0 copy-done
  1.7 0.0 copy-start.1
  1.7 1.0 copy-done.1
  2.7 0.0 copy-start.2
  2.7 1.0 copy-done.2
  3.8 0.0 copy-start.3
  3.8 1.0 copy-done.3
  4.8 0.0 copy-start.4
  4.8 0.7 copy-done.4
  5.5 0.0 copy-start.5
  5.5 0.7 copy-done.5
  6.2 0.0 copy-start.6
  6.2 0.7 copy-done.6
  6.8 82.0 %attend.1 = (bf16[16,256,128]{2,1,0:T(8,128)(2,1)S(1)}, f32[4096,128]{1,0:T(8,128)S(1)}, f32[128,128]{1,0:T(8,128)S(1)}, bf16[12288,128]{1,0:T(8,128)(2,1)S(1)}) custom-call(s32[2]{0:T(128)S(1)} %copy-done.6, s32[6,64]{1,0:T(8,128)S(1)} %bitcast.4, s32[6,64]{1,0:T(8,128)S(1)} %bitcast.6, bf16[256,1024]{1,0:T(8,128)(2,1)S(1)} %copy-done, ...), custom_call_target="tpu_custom_call" | custom-call | tf_op jit(solution)/shard_map/attend/pallas_call | solution.py:366
  88.9 3.5 %total.1 = (bf16[4096,128]{1,0:T(8,128)(2,1)S(1)}, bf16[256,1024]{1,0:T(8,128)(2,1)}, bf16[256,1024]{1,0:T(8,128)(2,1)}) custom-call(s32[2]{0:T(128)S(1)} %copy-done.6, s32[6,64]{1,0:T(8,128)S(1)} %bitcast.5, s32[6,64]{1,0:T(8,128)S(1)} %bitcast.7, f32[4096,128]{1,0:T(8,128)S(1)} %get-tuple-element.13.acc_in, f32[128,128]{1,0:T(8,128)S(1)} %get-tuple-element.14.glob_ref, ...), custom_call_target="tpu_custom_call" | custom-call | tf_op jit(solution)/shard_map/total/pallas_call | solution.py:392
  92.4 34.0 %back.1 = (bf16[256,1024]{1,0:T(8,128)(2,1)S(1)}, bf16[256,1024]{1,0:T(8,128)(2,1)S(1)}) custom-call(bf16[16,256,128]{2,1,0:T(8,128)(2,1)S(1)} %bitcast.3), custom_call_target="tpu_custom_call" | custom-call | tf_op jit(solution)/shard_map/back/pallas_call | solution.py:401
  126.4 0.8 copy.13
  127.2 0.8 copy.14
Async XLA Ops:
  0.6 1.0 copy-start
  1.7 1.0 copy-start.1
  2.7 1.0 copy-start.2
  3.8 1.0 copy-start.3
  4.8 0.7 copy-start.4
  5.5 0.7 copy-start.5
  6.2 0.7 copy-start.6
